TPU v7x, 32 devices: a whole 2x2x4 slice. The times are simulated.
32 devices in a mesh: dp: 4 (over y, core), seq: 8 (over z, x).
Axes of the slice: x: 2, y: 2, z: 4, core: 2. Of those that a mesh axis runs over, the one named last changes fastest.
Arguments:
- patches: bfloat16 [8192, 768], P(('dp', 'seq')), may hold values from -6 to 6
- cotangent: bfloat16 [8192, 768], P(('dp', 'seq')), may hold values from -6 to 6
- input_views: int32 [4], P('dp'), may hold values from 1 to 1, as said below
- token_live: int32 [8192], P(('dp', 'seq')), may hold values from 0 to 1, as said below
- master: float32 [768, 12, 768], P('dp', None, 'seq')
- moment_one: float32 [768, 12, 768], P('dp', None, 'seq')
- moment_two: float32 [768, 12, 768], P('dp', None, 'seq'), as said below
- norm_params: float32 [4, 768], replicated, as said below
- norm_moment_one: float32 [4, 768], replicated
- norm_moment_two: float32 [4, 768], replicated, as said below
Outputs:
- block_out: bfloat16 [8192, 768], P(('dp', 'seq'))
- patches_grad: float32 [8192, 768], P(('dp', 'seq'))
- new_master: float32 [768, 12, 768], P('dp', None, 'seq')
- new_copy: bfloat16 [768, 12, 768], P('dp', None, 'seq')
- new_moment_one: float32 [768, 12, 768], P('dp', None, 'seq')
- new_moment_two: float32 [768, 12, 768], P('dp', None, 'seq')
- new_norm_params: float32 [4, 768], replicated
- new_norm_moment_one: float32 [4, 768], replicated
- new_norm_moment_two: float32 [4, 768], replicated
- grad_norm: float32 [], replicated
Inputs may be any that keep to these rules, and one draw needn't show every extreme that they name: Scene g's first input_views[g] views are input views, the rest target views. `token_live`: the first patch of every view is present. `moment_two`: positive. `norm_params`: rows 0 and 2 are positive. `norm_moment_two`: positive.
All inputs are finite; a program needn't handle non-finite values.
Results may differ from a plain program's by a relative error of at most 0.017.
Values may be sent and summed in bfloat16 or wider, within the bound.
No kernel may reach another device: no remote copies, remote signals or barrier semaphores. Data moves between devices by JAX's collectives and lax.ppermute only.
A program may use at most 192 MiB of HBM per device.

v0:
```python
import math
from functools import partial

import jax
import jax.numpy as jnp
from jax import lax
from jax.experimental import pallas as pl
from jax.experimental.pallas import tpu as pltpu
from jax.sharding import PartitionSpec as P

D = 768
HEADS = 12
HEAD_DIM = 64
FF = 3072
VIEW = 1024
STEP = 10
GROUPS = 4
GROUP_HEADS = HEADS // GROUPS
GROUP_WIDTH = GROUP_HEADS * HEAD_DIM
WIDE = FF // D
RING = (0, 1, 3, 2)

layer_eps = 1e-05
beta_first = 0.9
beta_second = 0.95
adam_eps = 1e-08
rate_matrix = 0.08
rate_vector = 0.8
weight_decay = 0.1
masked_score = -1e30
bf16 = jnp.bfloat16
f32 = jnp.float32


def gray(v):
    return v ^ (v >> 1)


def hop_quarter(value, by):
    split = lax.axis_size("seq") // GROUPS
    pairs = [
        (RING[p] * split + x, RING[(p + by) % GROUPS] * split + x) for p in range(GROUPS) for x in range(split)
    ]
    return lax.ppermute(value, "seq", pairs)


def hop_within(value, by):
    split = lax.axis_size("seq") // GROUPS
    pairs = [(q * split + x, q * split + (x + by) % split) for q in range(GROUPS) for x in range(split)]
    return lax.ppermute(value, "seq", pairs)


def swap(value, axis, bit):
    return lax.ppermute(value, axis, [(i, i ^ bit) for i in range(lax.axis_size(axis))])


def bits_of(axis):
    return [1 << b for b in range(lax.axis_size(axis).bit_length() - 1)]


def total(value):
    for axis in ("dp", "seq"):
        for bit in bits_of(axis):
            value = value + swap(value, axis, bit)
    return value


def pick(stack, index):
    return lax.dynamic_index_in_dim(stack, index, 0, keepdims=False)


def layer_stats(values):
    centre = jnp.mean(values, axis=-1, keepdims=True)
    shifted = values - centre
    spread = jnp.mean(shifted * shifted, axis=-1, keepdims=True)
    inverse = lax.rsqrt(spread + layer_eps)
    return (shifted * inverse, inverse)


def layer_back(grad_normed, normalized, inverse, gain):
    scaled = grad_normed * gain
    centred = jnp.mean(scaled, axis=-1, keepdims=True)
    along = jnp.mean(scaled * normalized, axis=-1, keepdims=True)
    return inverse * (scaled - centred - normalized * along)


def mm(a, b):
    return jnp.dot(a, b, preferred_element_type=f32)


def mm_nt(a, b):
    return lax.dot_general(a, b, (((1,), (1,)), ((), ())), preferred_element_type=f32)


def mm_tn(a, b):
    return lax.dot_general(a, b, (((0,), (0,)), ((), ())), preferred_element_type=f32)


def gather_rows(piece):
    for bit in reversed(bits_of("dp")):
        piece = jnp.concatenate([piece, swap(piece, "dp", bit)], axis=1)
    return piece


def row_order():
    order = [0]
    for bit in reversed(bits_of("dp")):
        order = order + [o ^ bit for o in order]
    return order


def reduce_rows(piece):
    for bit in bits_of("dp"):
        half = piece.shape[1] // 2
        there = swap(piece[:, half:], "dp", bit)
        piece = (piece[:, :half].astype(f32) + there.astype(f32)).astype(bf16)
    return piece


def reduce_within(piece):
    own = piece[0].astype(f32)
    for j in range(1, piece.shape[0]):
        own = own + hop_within(piece[j], -j).astype(f32)
    return own.astype(bf16)


def reduce_ring(slots):
    moving = slots[1]
    for k in (2, 3):
        moving = (hop_quarter(moving, 1).astype(f32) + slots[k].astype(f32)).astype(bf16)
    return hop_quarter(moving, 1).astype(f32) + slots[0].astype(f32)


def adam_step(params, grads, first, second, rate, decay):
    first_new = beta_first * first + (1.0 - beta_first) * grads
    second_new = beta_second * second + (1.0 - beta_second) * grads * grads
    first_hat = first_new / (1.0 - beta_first**STEP)
    second_hat = second_new / (1.0 - beta_second**STEP)
    params_new = params - rate * (first_hat / (jnp.sqrt(second_hat) + adam_eps) + decay * params)
    return (params_new, first_new, second_new)


def relative(dp, absolute, order):
    index = jnp.int32(0)
    for at, offset in enumerate(order):
        index = jnp.where((dp ^ absolute) == offset, at, index)
    return index


def step_general(
    patches,
    cotangent,
    input_views,
    token_live,
    master,
    moment_one,
    moment_two,
    norm_params,
    norm_moment_one,
    norm_moment_two,
):
    tokens = patches.shape[0]
    rows, blocks, cols = master.shape
    n_dp = lax.axis_size("dp")
    split = lax.axis_size("seq") // GROUPS
    dp = lax.axis_index("dp")
    seq = lax.axis_index("seq")
    quarter, within = seq // split, seq % split
    place = gray(quarter)
    inputs_seen = input_views[0]
    gain_one, shift_one, gain_two, shift_two = (norm_params[i] for i in range(4))
    order = row_order()
    dp_place = [order.index(a) for a in range(n_dp)]

    def quarter_behind(k):
        return gray((place - k) & 3)

    flags = jnp.pad(token_live.astype(bf16)[None, :], ((0, 7), (0, D - tokens)))
    ring = [jnp.concatenate([patches, flags], axis=0)]
    for _ in range(3):
        ring.append(hop_quarter(ring[-1], 1))
    pieces = [[ring[k]] + [hop_within(ring[k], j) for j in range(1, split)] for k in range(4)]
    scene = jnp.stack([jnp.stack([p[:tokens] for p in pieces[k]]) for k in range(4)])
    live = jnp.stack([jnp.concatenate([p[tokens, :tokens] for p in pieces[k]]) for k in range(4)])

    copy_low = master.astype(bf16)
    mine = copy_low[:, 0:3, :].reshape(rows, 3 * cols)
    near = jnp.stack([mine] + [hop_within(mine, j) for j in range(1, split)])
    near = gather_rows(near).reshape(split, n_dp, rows, 3, cols)
    near = jnp.stack([pick(near, (within - a) % split) for a in range(split)])
    near = jnp.moveaxis(near, 1, 0)
    near = jnp.stack([pick(near, order_at) for order_at in [relative(dp, a, order) for a in range(n_dp)]])
    w_qkv = jnp.transpose(near, (0, 2, 3, 1, 4)).reshape(D, 3, GROUP_WIDTH)

    up = copy_low[:, 4 : 4 + WIDE].reshape(rows, WIDE * cols)
    down = copy_low[:, 4 + WIDE :].reshape(rows, WIDE * cols)
    far = [jnp.concatenate([up, down, copy_low[:, 3]], axis=1)]
    for _ in range(3):
        far.append(hop_quarter(far[-1], 1))
    weights = [gather_rows(jnp.stack([f] + [hop_within(f, j) for j in range(1, split)])) for f in far]
    width = WIDE * cols
    w_up = [w[:, :, :width] for w in weights]
    w_down = [w[:, :, width : 2 * width] for w in weights]
    w_out = jnp.stack([w[:, :, 2 * width :] for w in weights]).reshape(4 * split, n_dp, rows, cols)

    def slot_of(quarter_abs, within_abs):
        return ((place - gray(quarter_abs)) & 3) * split + (within - within_abs) % split

    w_out = jnp.stack([pick(w_out, slot_of(a // split, a % split)) for a in range(4 * split)])
    w_out = jnp.moveaxis(w_out, 1, 0)
    w_out = jnp.stack([pick(w_out, relative(dp, a, order)) for a in range(n_dp)])
    w_out = jnp.transpose(w_out, (0, 2, 1, 3)).reshape(D, D)

    normal_one, inverse_one = layer_stats(scene.astype(f32))
    act_one = (normal_one * gain_one + shift_one).astype(bf16)
    act_all = act_one.reshape(4 * split * tokens, D)
    act_own = act_one[:, 0].reshape(4 * tokens, D)
    q = mm(act_own, w_qkv[:, 0]).astype(bf16)
    k = mm(act_all, w_qkv[:, 1]).astype(bf16)
    v = mm(act_all, w_qkv[:, 2]).astype(bf16)

    def heads(m):
        return jnp.transpose(m.reshape(m.shape[0], GROUP_HEADS, HEAD_DIM), (1, 0, 2))

    def unheads(m):
        return jnp.transpose(m, (1, 0, 2)).reshape(m.shape[1], GROUP_WIDTH)

    views = jnp.stack([(quarter_behind(i) * split * tokens) // VIEW for i in range(4)])
    open_block = (views[None, :] < inputs_seen) | (views[None, :] == views[:, None])
    visible = open_block[:, None, :, None] & (live > 0)[None, None]
    visible = jnp.broadcast_to(visible, (4, tokens, 4, split * tokens)).reshape(4 * tokens, -1)
    scaling = 1.0 / math.sqrt(HEAD_DIM)
    qh, kh, vh = heads(q), heads(k), heads(v)
    scores = jnp.einsum("hqd,hkd->hqk", qh, kh, preferred_element_type=f32) * scaling
    scores = jnp.where(visible[None], scores, masked_score)
    top = jnp.max(scores, axis=-1, keepdims=True)
    probs = jnp.where(visible[None], jnp.exp(scores - top), 0.0)
    probs = probs / jnp.sum(probs, axis=-1, keepdims=True)
    probs_low = probs.astype(bf16)
    attended = jnp.einsum("hqk,hkd->hqd", probs_low, vh, preferred_element_type=f32)
    flat = unheads(attended).astype(bf16).reshape(4, tokens, GROUP_WIDTH)
    back = jnp.stack([flat[0]] + [hop_quarter(flat[i], -i) for i in range(1, 4)])
    act_two = jnp.concatenate([pick(back, (gray(a) - place) & 3) for a in range(4)], axis=1)

    patch_float = patches.astype(f32)
    resid = patch_float + mm(act_two, w_out)
    normal_two, inverse_two = layer_stats(resid)
    act_three = (normal_two * gain_two + shift_two).astype(bf16)

    def to_relative(m):
        parts = m.reshape(tokens, n_dp, rows)
        return jnp.concatenate([lax.dynamic_index_in_dim(parts, dp ^ o, 1, keepdims=False) for o in order], axis=1)

    def from_relative(m):
        parts = m.reshape(tokens, n_dp, rows)
        return jnp.concatenate(
            [lax.dynamic_index_in_dim(parts, relative(dp, a, order), 1, keepdims=False) for a in range(n_dp)], axis=1
        )

    act_rel = to_relative(act_three)
    cot_rel = to_relative(cotangent)
    branch_rel = jnp.zeros((tokens, D), f32)
    three_rel = jnp.zeros((tokens, D), f32)
    far_grads = []
    for i in range(4):
        group = []
        for j in range(split):
            widened = mm(act_rel, w_up[i][j])
            activated, gelu_pull = jax.vjp(partial(jax.nn.gelu, approximate=False), widened)
            hidden = activated.astype(bf16)
            branch_rel = branch_rel + mm_nt(hidden, w_down[i][j])
            grad_wide = gelu_pull(mm(cot_rel, w_down[i][j]))[0].astype(bf16)
            three_rel = three_rel + mm_nt(grad_wide, w_up[i][j])
            grad_up = mm_tn(act_rel, grad_wide).astype(bf16)
            grad_down = mm_tn(cot_rel, hidden).astype(bf16)
            group.append((grad_up, grad_down))
        far_grads.append(group)
    block_out = (resid + from_relative(branch_rel)).astype(bf16)
    grad_three = from_relative(three_rel)
    gain_two_grad = jnp.sum(grad_three * normal_two, axis=0)
    shift_two_grad = jnp.sum(grad_three, axis=0)
    grad_resid = cotangent.astype(f32) + layer_back(grad_three, normal_two, inverse_two, gain_two)
    grad_branch = grad_resid.astype(bf16)
    grad_attended = mm_nt(grad_branch, w_out).astype(bf16)
    grad_w_out = mm_tn(act_two, grad_branch).astype(bf16)

    parts = jnp.transpose(grad_attended.reshape(tokens, 4, GROUP_WIDTH), (1, 0, 2))
    parts = [pick(parts, gray((place + i) & 3)) for i in range(4)]
    grad_here = jnp.concatenate([parts[0]] + [hop_quarter(parts[i], i) for i in range(1, 4)], axis=0)
    gh = heads(grad_here)
    dprobs = jnp.einsum("hqd,hkd->hqk", gh, vh, preferred_element_type=f32)
    delta = jnp.sum(gh.astype(f32) * attended, axis=-1, keepdims=True)
    grad_scores = (probs * (dprobs - delta)).astype(bf16)
    dq = unheads(jnp.einsum("hqk,hkd->hqd", grad_scores, kh, preferred_element_type=f32) * scaling).astype(bf16)
    dk = unheads(jnp.einsum("hqk,hqd->hkd", grad_scores, qh, preferred_element_type=f32) * scaling).astype(bf16)
    dv = unheads(jnp.einsum("hqk,hqd->hkd", probs_low, gh, preferred_element_type=f32)).astype(bf16)

    grad_near = jnp.stack([mm_tn(act_own, dq), mm_tn(act_all, dk), mm_tn(act_all, dv)], axis=1).astype(bf16)
    grad_near = grad_near.reshape(n_dp, rows, 3, split, cols)
    grad_near = jnp.stack([pick(grad_near, dp ^ o) for o in order])
    grad_near = jnp.transpose(grad_near, (3, 0, 1, 2, 4)).reshape(split, D, 3 * cols)
    grad_near = jnp.stack([pick(grad_near, (within - j) % split) for j in range(split)])
    grad_near = reduce_within(reduce_rows(grad_near)).astype(f32).reshape(rows, 3, cols)

    one_q = mm_nt(dq, w_qkv[:, 0]).reshape(4, 1, tokens, D)
    one_kv = (mm_nt(dk, w_qkv[:, 1]) + mm_nt(dv, w_qkv[:, 2])).reshape(4, split, tokens, D)
    one = jnp.concatenate([one_kv[:, :1] + one_q, one_kv[:, 1:]], axis=1)
    gain_one_grad = jnp.sum(one * normal_one, axis=(0, 1, 2))
    shift_one_grad = jnp.sum(one, axis=(0, 1, 2))
    one_low = one.astype(bf16)
    grad_one = reduce_ring([reduce_within(one_low[i]) for i in range(4)])
    patches_grad = grad_resid + layer_back(grad_one, normal_one[0, 0], inverse_one[0, 0], gain_one)

    out_parts = grad_w_out.reshape(n_dp, rows, 4 * split, cols)
    out_parts = jnp.stack([pick(out_parts, dp ^ o) for o in order])
    out_parts = jnp.transpose(out_parts, (2, 0, 1, 3)).reshape(4 * split, D, cols)
    slots = []
    for i in range(4):
        stack = []
        for j in range(split):
            own_out = pick(out_parts, quarter_behind(i) * split + (within - j) % split)
            stack.append(jnp.concatenate([*far_grads[i][j], own_out], axis=1))
        slots.append(reduce_within(reduce_rows(jnp.stack(stack))))
    far_sum = reduce_ring(slots)
    grad_up = far_sum[:, :width].reshape(rows, WIDE, cols)
    grad_down = far_sum[:, width : 2 * width].reshape(rows, WIDE, cols)
    grad_out = far_sum[:, 2 * width :].reshape(rows, 1, cols)

    weight_grad = jnp.concatenate([grad_near, grad_out, grad_up, grad_down], axis=1)
    param_grad = total(jnp.stack([gain_one_grad, shift_one_grad, gain_two_grad, shift_two_grad]))
    squares = total(jnp.full((8, 128), jnp.sum(weight_grad * weight_grad), f32))[0, 0] + jnp.sum(param_grad * param_grad)
    grad_norm = jnp.sqrt(squares)
    clip = 1.0 / jnp.maximum(grad_norm, 1.0)
    new_master, new_moment_one, new_moment_two = adam_step(
        master, weight_grad * clip, moment_one, moment_two, rate_matrix, weight_decay
    )
    new_norm_params, new_norm_moment_one, new_norm_moment_two = adam_step(
        norm_params, param_grad * clip, norm_moment_one, norm_moment_two, rate_vector, 0.0
    )
    return (
        block_out,
        patches_grad,
        new_master,
        new_master.astype(bf16),
        new_moment_one,
        new_moment_two,
        new_norm_params,
        new_norm_moment_one,
        new_norm_moment_two,
        grad_norm,
    )


HALF = 48
ANY = pl.BlockSpec(memory_space=pl.ANY)
SMEM = pl.BlockSpec(memory_space=pltpu.SMEM)
VMEM_LIMIT = 56 << 20
SCALE = 1.0


def call(body, name, ins, outs, operands, scratch=(), us=4, out_specs=None, aliases=None):
    return pl.pallas_call(
        body,
        name=name,
        out_shape=outs,
        in_specs=ins,
        out_specs=out_specs or jax.tree.map(lambda _: pl.BlockSpec(memory_space=pltpu.VMEM), outs),
        scratch_shapes=list(scratch),
        input_output_aliases=aliases or {},
        cost_estimate=pl.CostEstimate(flops=int(us * SCALE * 1e9), bytes_accessed=int(us * SCALE * 3.6e6), transcendentals=0),
        compiler_params=pltpu.CompilerParams(vmem_limit_bytes=VMEM_LIMIT),
    )(*operands)


VM = pl.BlockSpec(memory_space=pltpu.VMEM)


def shape(dims, dtype):
    return jax.ShapeDtypeStruct(dims, dtype)


def run_copies(copies):
    for c in copies:
        c.start()
    for c in copies:
        c.wait()


def place_qkv(at, own_half, other_half):
    def body(at_ref, own_ref, other_ref, out_ref, sems):
        x, y, c = at_ref[0], at_ref[1], at_ref[2]
        copies = []
        for block in range(3):
            for j in range(2):
                for r in range(2):
                    for h, ref in ((0, own_ref), (1, other_ref)):
                        row = block * GROUP_WIDTH + (x ^ j) * 96 + (c ^ h) * HALF
                        copies.append(
                            pltpu.make_async_copy(
                                ref.at[r, j, pl.ds(block * HALF, HALF), :],
                                out_ref.at[
                                    pl.ds(pl.multiple_of(row, 16), HALF),
                                    pl.ds(pl.multiple_of((y ^ r) * 384, 128), 384),
                                ],
                                sems.at[len(copies)],
                            )
                        )
        run_copies(copies)

    return call(
        body,
        "place_qkv",
        [SMEM, ANY, ANY],
        shape((3 * GROUP_WIDTH, D), bf16),
        (at, own_half, other_half),
        [pltpu.SemaphoreType.DMA((24,))],
    )


def place_out(at, own_half, other_half):
    def body(at_ref, own_ref, other_ref, out_ref, sems):
        x, y, c, place = at_ref[0], at_ref[1], at_ref[2], at_ref[3]
        copies = []
        for k in range(4):
            quarter = gray((place - k) & 3)
            for j in range(2):
                for r in range(2):
                    for h, ref in ((0, own_ref), (1, other_ref)):
                        row = (quarter * 2 + (x ^ j)) * 96
                        copies.append(
                            pltpu.make_async_copy(
                                ref.at[r, k * 2 + j],
                                out_ref.at[(y ^ r) * 2 + (c ^ h), pl.ds(pl.multiple_of(row, 16), 96), :],
                                sems.at[len(copies)],
                            )
                        )
        run_copies(copies)

    return call(
        body,
        "place_out",
        [SMEM, ANY, ANY],
        shape((4, D, 256), bf16),
        (at, own_half, other_half),
        [pltpu.SemaphoreType.DMA((32,))],
        us=3,
    )


def normalize(values):
    centre = jnp.mean(values, axis=-1, keepdims=True)
    shifted = values - centre
    inverse = lax.rsqrt(jnp.mean(shifted * shifted, axis=-1, keepdims=True) + layer_eps)
    return shifted * inverse, inverse


def lane_index(dims):
    return lax.broadcasted_iota(jnp.int32, dims, len(dims) - 1)


def project(first, second, w_t, norms):
    def body(a_ref, b_ref, w_ref, norm_ref, act_ref, normal_ref, q_ref, k_ref, v_ref, wide_ref):
        wide_ref[...] = jnp.zeros_like(wide_ref)
        for h in range(9):
            wide_ref[h * 128 : h * 128 + 64, :] = w_ref[h * 64 : h * 64 + 64, :]
        gain, shift = norm_ref[0:1, :], norm_ref[1:2, :]
        for piece, ref in enumerate((a_ref, b_ref)):
            at = slice(piece * 256, piece * 256 + 256)
            normal, _ = normalize(ref[0:256, :].astype(f32))
            act = (normal * gain + shift).astype(bf16)
            normal_ref[at, :] = normal.astype(bf16)
            act_ref[at, :] = act
            flags = ref[256:257, 0:256].astype(f32)
            mask = jnp.where(flags > 0, 0.0, masked_score)
            mask = jnp.transpose(jnp.broadcast_to(mask, (128, 256)))
            lanes = lane_index((256, 128))
            for h in range(3):
                if piece == 0:
                    q = mm_nt(act, wide_ref[h * 128 : h * 128 + 128, :]).astype(bf16).astype(f32)
                    q = jnp.where(lanes == 64, 1.0, q * (1.0 / math.sqrt(HEAD_DIM)))
                    q_ref[h] = q.astype(bf16)
                k = mm_nt(act, wide_ref[(3 + h) * 128 : (4 + h) * 128, :])
                k = jnp.where(lanes == 64, mask, k)
                k_ref[h, at, :] = jnp.where((lanes > 64) & (lanes < 68), 1.0, k).astype(bf16)
                v = mm_nt(act, wide_ref[(6 + h) * 128 : (7 + h) * 128, :])
                v_ref[h, at, :] = jnp.where((lanes > 63) & (lanes < 67), 1.0, v).astype(bf16)

    outs = [
        shape((512, D), bf16),
        shape((512, D), bf16),
        shape((3, 256, 128), bf16),
        shape((3, 512, 128), bf16),
        shape((3, 512, 128), bf16),
    ]
    return call(body, "norm_project", [VM] * 4, outs, (first, second, w_t, norms), [pltpu.VMEM((1152, D), bf16)], us=4)


def in_three(value):
    high = value.astype(bf16).astype(f32)
    rest = value - high
    mid = rest.astype(bf16).astype(f32)
    return high, mid, rest - mid


def with_parts(base, lanes, first, value):
    for i, part in enumerate(in_three(value)):
        base = jnp.where(lanes == first + i, part, base)
    return base


def join_heads(parts):
    return jnp.concatenate([p[:, :HEAD_DIM] for p in parts], axis=1)


def stack_slots(place, slots, stacked, sems, base=0):
    return [
        pltpu.make_async_copy(ref, stacked.at[gray((place - k) & 3)], sems.at[base + k]) for k, ref in enumerate(slots)
    ]


def attend(at, qs, ks, vs):
    def body(at_ref, *refs):
        low_refs, full_ref, back_ref = refs[12:16], refs[16], refs[17]
        q_ref, k_ref, v_ref, sems = refs[18:22]
        place = at_ref[3]
        lanes = lane_index((256, 128))
        run_copies(
            stack_slots(place, refs[0:4], q_ref, sems)
            + stack_slots(place, refs[4:8], k_ref, sems, 4)
            + stack_slots(place, refs[8:12], v_ref, sems, 8)
        )

        def head(h, _):
            for i in range(4):
                chunks = (0, 1) if i < 2 else (0, 1, 2, 3)
                q = q_ref[i, h]
                scores = [mm_nt(q, k_ref[c, h]) for c in chunks]
                top = None
                for s in scores:
                    for b in range(0, s.shape[1], 128):
                        part = s[:, b : b + 128]
                        top = part if top is None else jnp.maximum(top, part)
                top = jnp.max(top, axis=1, keepdims=True)
                mixed = None
                for s, c in zip(scores, chunks):
                    part = mm(jnp.exp(s - top).astype(bf16), v_ref[c, h])
                    mixed = part if mixed is None else mixed + part
                norm = mixed[:, HEAD_DIM : HEAD_DIM + 1]
                full_ref[i, h] = mixed / norm
                logsum = top + jnp.log(norm)
                back_ref[i, h] = with_parts(q.astype(f32), lanes, 65, -logsum).astype(bf16)
            return 0

        lax.fori_loop(0, 3, head, 0)
        for k in range(4):
            i = gray((place - k) & 3)
            low_refs[k][...] = join_heads([full_ref[i, h] for h in range(3)]).astype(bf16)

    outs = (
        [shape((256, GROUP_WIDTH), bf16)] * 4 + [shape((4, 3, 256, 128), f32)] + [shape((4, 3, 256, 128), bf16)]
    )
    got = call(
        body,
        "attend",
        [SMEM] + [ANY] * 12,
        outs,
        (at, *qs, *ks, *vs),
        [
            pltpu.VMEM((4, 3, 256, 128), bf16),
            pltpu.VMEM((4, 3, 512, 128), bf16),
            pltpu.VMEM((4, 3, 512, 128), bf16),
            pltpu.SemaphoreType.DMA((12,)),
        ],
        us=12,
    )
    return got[0:4], got[4], got[5]


def attend_back(at, q_back, ks, vs, full, grads):
    def body(at_ref, q_ref, *refs):
        full_ref, g_refs = refs[8], refs[9:13]
        dq_refs, dk_refs, dv_refs = refs[13:17], refs[17:21], refs[21:25]
        k_ref, v_ref, g_ref, dq_ref, dk_ref, dv_ref, sems = refs[25:32]
        place = at_ref[3]
        copies = stack_slots(place, refs[0:4], k_ref, sems) + stack_slots(place, refs[4:8], v_ref, sems, 4)
        for c in copies:
            c.start()
        lanes = lane_index((256, 128))
        for k in range(4):
            i = gray((place - k) & 3)
            for h in range(3):
                g = g_refs[k][:, h * 64 : h * 64 + 64].astype(f32)
                delta = jnp.sum(g * full_ref[i, h][:, :64], axis=-1, keepdims=True)
                g = jnp.concatenate([g, jnp.zeros((256, 64), f32)], axis=1)
                g_ref[h, pl.ds(pl.multiple_of(i * 256, 256), 256), :] = with_parts(g, lanes, 64, -delta).astype(bf16)
        for c in copies:
            c.wait()

        def head(h, _):
            q_all = jnp.concatenate([q_ref[i, h] for i in range(4)], axis=0)
            for c in range(4):
                first = 0 if c < 2 else 512
                k, v = k_ref[c, h], v_ref[c, h]
                q, g = q_all[first:], g_ref[h, first:, :]
                p = jnp.exp(mm_nt(k, q))
                ds = (p * mm_nt(v, g)).astype(bf16)
                dv_ref[c, h] = mm(p.astype(bf16), g)
                dk_ref[c, h] = mm(ds, q)
                dq = mm(jnp.transpose(k), ds)
                if c == 0:
                    dq_ref[h] = dq
                else:
                    dq_ref[h, :, first:] += dq
            return 0

        lax.fori_loop(0, 3, head, 0)
        for k in range(4):
            i = gray((place - k) & 3)
            cols = pl.ds(pl.multiple_of(i * 256, 256), 256)
            parts = [jnp.transpose(dq_ref[h, :, cols]) for h in range(3)]
            dq_refs[k][...] = (join_heads(parts) * (1.0 / math.sqrt(HEAD_DIM))).astype(bf16)
            dk_refs[k][...] = join_heads([dk_ref[i, h] for h in range(3)]).astype(bf16)
            dv_refs[k][...] = join_heads([dv_ref[i, h] for h in range(3)]).astype(bf16)

    outs = [shape((256, GROUP_WIDTH), bf16)] * 4 + [shape((512, GROUP_WIDTH), bf16)] * 8
    got = call(
        body,
        "attend_back",
        [SMEM, VM] + [ANY] * 8 + [VM] * 5,
        outs,
        (at, q_back, *ks, *vs, full, *grads),
        [
            pltpu.VMEM((4, 3, 512, 128), bf16),
            pltpu.VMEM((4, 3, 512, 128), bf16),
            pltpu.VMEM((3, 1024, 128), bf16),
            pltpu.VMEM((3, 128, 1024), f32),
            pltpu.VMEM((4, 3, 512, 128), f32),
            pltpu.VMEM((4, 3, 512, 128), f32),
            pltpu.SemaphoreType.DMA((8,)),
        ],
        us=16,
    )
    return got[0:4], got[4:8], got[8:12]


def input_back(normals, dqs, dks, dvs, w_t):
    count = len(normals)

    def body(*refs):
        normal_refs, dq_refs, dk_refs, dv_refs = (refs[n * count : (n + 1) * count] for n in range(4))
        w_ref, *outs = refs[4 * count :]
        keep_refs, send_refs, norm_ref = outs[0:count], outs[count : 2 * count], outs[2 * count]
        gains, shifts = jnp.zeros((1, D), f32), jnp.zeros((1, D), f32)
        for i in range(count):
            for j, out_ref in enumerate((keep_refs[i], send_refs[i])):
                r = slice(j * 256, j * 256 + 256)
                one = mm(dk_refs[i][r, :], w_ref[192:384, :]) + mm(dv_refs[i][r, :], w_ref[384:576, :])
                if j == 0:
                    one = one + mm(dq_refs[i][...], w_ref[0:192, :])
                gains = gains + jnp.sum(one * normal_refs[i][r, :].astype(f32), axis=0, keepdims=True)
                shifts = shifts + jnp.sum(one, axis=0, keepdims=True)
                out_ref[...] = one.astype(bf16)
        norm_ref[...] = jnp.concatenate([gains, shifts, jnp.zeros((6, D), f32)], axis=0)

    outs = [shape((256, D), bf16)] * (2 * count) + [shape((8, D), f32)]
    got = call(body, "input_back", [VM] * (4 * count + 1), outs, (*normals, *dqs, *dks, *dvs, w_t), us=count + 1)
    return got[0:count], got[count : 2 * count], got[2 * count]


def projections_back(at, acts, dqs, dks, dvs):
    def body(at_ref, *refs):
        act_refs, dq_refs, dk_refs, dv_refs = (refs[4 * n : 4 * n + 4] for n in range(4))
        w_keep_ref, w_send_ref, dw_ref = refs[16:19]
        for i in range(4):
            act = act_refs[i][...]
            for b, (ref, rows) in enumerate(((dq_refs[i], 256), (dk_refs[i], 512), (dv_refs[i], 512))):
                part = mm_tn(ref[...], act[:rows])
                at_rows = slice(b * GROUP_WIDTH, (b + 1) * GROUP_WIDTH)
                dw_ref[at_rows, :] = part if i == 0 else dw_ref[at_rows, :] + part
        x, c = at_ref[0], at_ref[2]
        for b in range(3):
            for xa in range(2):
                for half in range(2):
                    row = b * GROUP_WIDTH + (xa * 2 + half) * HALF
                    block = dw_ref[row : row + HALF, :].astype(bf16)

                    @pl.when(c == half)
                    def _():
                        w_keep_ref[(x ^ xa) * 3 + b] = block

                    @pl.when(c != half)
                    def _():
                        w_send_ref[(x ^ xa) * 3 + b] = block

    return call(
        body,
        "projections_back",
        [SMEM] + [VM] * 16,
        [shape((6, HALF, D), bf16)] * 2,
        (at, *acts, *dqs, *dks, *dvs),
        [pltpu.VMEM((3 * GROUP_WIDTH, D), f32)],
        us=6,
    )


def out_norm(at, patches, mixed, w_out, norms):
    def body(at_ref, x_ref, m0, m1, m2, m3, w_ref, norm_ref, two_ref, resid_ref, normal_ref, inverse_ref, three_ref):
        place = at_ref[3]
        parts = [m[...].astype(f32) for m in (m0, m1, m2, m3)]
        groups = []
        for a in range(4):
            steps = (gray(a) - place) & 3
            part = parts[0]
            for k in (1, 2, 3):
                part = jnp.where(steps == k, parts[k], part)
            groups.append(part)
        resid = x_ref[...].astype(f32)
        for a in range(4):
            resid = resid + mm_nt(groups[a].astype(bf16), w_ref[a][:, :GROUP_WIDTH])
        two_ref[...] = jnp.concatenate(groups, axis=1).astype(bf16)
        resid_ref[...] = resid
        normal, inverse = normalize(resid)
        normal_ref[...] = normal
        inverse_ref[...] = jnp.broadcast_to(inverse, (256, 128))
        three_ref[...] = (normal * norm_ref[2:3, :] + norm_ref[3:4, :]).astype(bf16)

    outs = [
        shape((256, D), bf16),
        shape((256, D), f32),
        shape((256, D), f32),
        shape((256, 128), f32),
        shape((256, D), bf16),
    ]
    return call(body, "out_norm", [SMEM] + [VM] * 7, outs, (at, patches, *mixed, w_out, norms))


def by_core_rows(values):
    return jnp.concatenate([values[:, n * 192 : n * 192 + 192] for n in (0, 2, 1, 3)], axis=1)


def mlp(at, act, cot, weights, out_dtype):
    def body(at_ref, a_ref, c_ref, *refs):
        w_refs = refs[0:4]
        hidden_ref, wide_ref, out_ref, three_ref, act_ref, cot_ref, w_ref, out_acc, three_acc, sems = refs[4:14]
        core = at_ref[2]
        own_lanes = pl.ds(pl.multiple_of(core * 384, 128), 384)
        other_lanes = pl.ds(pl.multiple_of((1 - core) * 384, 128), 384)
        copies = []
        for k in range(4):
            group = []
            for r, lanes in enumerate((own_lanes, other_lanes)):
                for j in range(2):
                    for u in range(2):
                        group.append(
                            pltpu.make_async_copy(
                                w_refs[2 * r + k // 2].at[2 * (k % 2) + j, pl.ds(u * 192, 192), :],
                                w_ref.at[k, u, pl.ds(j * 192, 192), lanes],
                                sems.at[k, len(group)],
                            )
                        )
            copies.append(group)
            for c in group:
                c.start()
        act_ref[...] = by_core_rows(a_ref[...])
        cot_ref[...] = by_core_rows(c_ref[...])
        for k in range(4):
            for c in copies[k]:
                c.wait()
            up, down = w_ref[k, 0], w_ref[k, 1]
            widened = mm_nt(act_ref[...], up)
            inner = 0.5 * (1.0 + lax.erf(widened * (1.0 / math.sqrt(2.0))))
            slope = inner + widened * jnp.exp(-0.5 * widened * widened) * (1.0 / math.sqrt(2.0 * math.pi))
            hidden = (widened * inner).astype(bf16)
            wide = (mm_nt(cot_ref[...], down) * slope).astype(bf16)
            hidden_ref[:, k * 384 : k * 384 + 384] = hidden
            wide_ref[:, k * 384 : k * 384 + 384] = wide
            out, three = mm(hidden, down), mm(wide, up)
            out_acc[...] = out if k == 0 else out_acc[...] + out
            three_acc[...] = three if k == 0 else three_acc[...] + three
        out_ref[...] = by_core_rows(out_acc[...]).astype(out_dtype)
        three_ref[...] = by_core_rows(three_acc[...]).astype(out_dtype)

    return call(
        body,
        "mlp",
        [SMEM] + [VM] * 2 + [ANY] * 4,
        [shape((256, 1536), bf16)] * 2 + [shape((256, D), out_dtype)] * 2,
        (at, act, cot, *weights),
        [
            pltpu.VMEM((256, D), bf16),
            pltpu.VMEM((256, D), bf16),
            pltpu.VMEM((4, 2, 384, D), bf16),
            pltpu.VMEM((256, D), f32),
            pltpu.VMEM((256, D), f32),
            pltpu.SemaphoreType.DMA((4, 8)),
        ],
        us=8,
    )


def mlp_weights(at, acts, cots, hiddens, wides, slots):
    count = len(slots)

    def body(at_ref, *refs):
        a_refs, c_refs, h_refs, w_refs = (refs[2 * n : 2 * n + 2] for n in range(4))
        keep_ref, send_ref, act_ref, cot_ref, in_ref, stage_ref, in_sems, out_sems = refs[8:16]
        arriving = []
        for n, k in enumerate(slots):
            group = []
            for which, sources in enumerate((w_refs, h_refs)):
                for i in range(2):
                    group.append(
                        pltpu.make_async_copy(
                            sources[i].at[:, pl.ds(k * 384, 384)],
                            in_ref.at[n, which, pl.ds(i * 256, 256), :],
                            in_sems.at[n, len(group)],
                        )
                    )
                    group[-1].start()
            arriving.append(group)
        for i in range(2):
            act_ref[i * 256 : i * 256 + 256, :] = by_core_rows(a_refs[i][...])
            cot_ref[i * 256 : i * 256 + 256, :] = by_core_rows(c_refs[i][...])
        core = at_ref[2]
        own_lanes = pl.ds(pl.multiple_of(core * 384, 128), 384)
        other_lanes = pl.ds(pl.multiple_of((1 - core) * 384, 128), 384)
        leaving = []
        for n in range(count):
            for c in arriving[n]:
                c.wait()
            up = mm_tn(in_ref[n, 0], act_ref[...]).astype(bf16)
            down = mm_tn(in_ref[n, 1], cot_ref[...]).astype(bf16)
            for j in range(2):
                stage_ref[n, j, 0:192, :] = up[j * 192 : j * 192 + 192]
                stage_ref[n, j, 192:384, :] = down[j * 192 : j * 192 + 192]
            for i, (lanes, ref) in enumerate(((own_lanes, keep_ref), (other_lanes, send_ref))):
                leaving.append(pltpu.make_async_copy(stage_ref.at[n, :, :, lanes], ref.at[:, n], out_sems.at[n, i]))
                leaving[-1].start()
        for c in leaving:
            c.wait()

    return call(
        body,
        "mlp_weights",
        [SMEM] + [VM] * 4 + [ANY] * 4,
        [shape((2, count, 384, 384), bf16)] * 2,
        (at, *acts, *cots, *hiddens, *wides),
        [
            pltpu.VMEM((512, D), bf16),
            pltpu.VMEM((512, D), bf16),
            pltpu.VMEM((count, 2, 512, 384), bf16),
            pltpu.VMEM((count, 2, 384, D), bf16),
            pltpu.SemaphoreType.DMA((count, 4)),
            pltpu.SemaphoreType.DMA((count, 2)),
        ],
        us=4,
        out_specs=[ANY] * 2,
    )


def norm_out_back(at, three, three_there, cotangent, normal, inverse, two, w_out, norms):
    def body(at_ref, t_ref, s_ref, c_ref, n_ref, i_ref, two_ref, w_ref, norm_ref, *outs):
        resid_ref, sums_ref = outs[0:2]
        g_refs, keep_ref, send_ref, dw_ref = outs[2:6], outs[6], outs[7], outs[8]
        x, c, place = at_ref[0], at_ref[2], at_ref[3]
        grad = t_ref[...] + s_ref[...].astype(f32)
        normal = n_ref[...]
        sums_ref[...] = jnp.concatenate(
            [jnp.sum(grad * normal, axis=0, keepdims=True), jnp.sum(grad, axis=0, keepdims=True), jnp.zeros((6, D), f32)],
            axis=0,
        )
        resid = c_ref[...].astype(f32) + layer_back(grad, normal, i_ref[:, 0:1], norm_ref[2:3, :])
        resid_ref[...] = resid
        low = resid.astype(bf16)
        groups = [mm(low, w_ref[a][:, :GROUP_WIDTH]) for a in range(4)]
        for k in range(4):
            ahead = gray((place + k) & 3)
            part = groups[0]
            for a in (1, 2, 3):
                part = jnp.where(ahead == a, groups[a], part)
            g_refs[k][...] = part.astype(bf16)
        dw_ref[...] = mm_tn(low, two_ref[...])
        for q in range(4):
            for xa in range(2):
                slot = ((place - gray(q)) & 3) * 2 + (x ^ xa)
                for half in range(2):
                    row = (q * 2 + xa) * 96 + half * HALF
                    block = dw_ref[row : row + HALF, :].astype(bf16)

                    @pl.when(c == half)
                    def _():
                        keep_ref[slot] = block

                    @pl.when(c != half)
                    def _():
                        send_ref[slot] = block

    outs = (
        [shape((256, D), f32), shape((8, D), f32)]
        + [shape((256, GROUP_WIDTH), bf16)] * 4
        + [shape((8, HALF, D), bf16)] * 2
    )
    got = call(
        body,
        "norm_out_back",
        [SMEM] + [VM] * 8,
        outs,
        (at, three, three_there, cotangent, normal, inverse, two, w_out, norms),
        [pltpu.VMEM((D, D), f32)],
    )
    return got[0], got[1], got[2:6], got[6], got[7]


FAR_AFTER = 3


def after(value, *others):
    return lax.optimization_barrier((value, *others))[0]


def turn(at, far_own, far_there, near_own, near_there):
    def body(at_ref, far_own_ref, far_there_ref, near_own_ref, near_there_ref, out_ref):
        def write_far(refs):
            for half, ref in enumerate(refs):
                for u in range(2):
                    for j in range(2):
                        row = u * 192 + j * 96
                        out_ref[4 + 4 * u + 2 * half + j] = jnp.transpose(ref[row : row + 96, :].astype(f32))

        def write_near(refs):
            for b in range(4):
                rows = slice(b * HALF, (b + 1) * HALF)
                block = jnp.concatenate([ref[rows, :].astype(f32) for ref in refs], axis=0)
                out_ref[b] = jnp.transpose(block)

        for value in range(2):

            @pl.when(at_ref[1] == value)
            def _():
                write_far((far_own_ref, far_there_ref)[:: 1 if value == 0 else -1])

            @pl.when(at_ref[2] == value)
            def _():
                write_near((near_own_ref, near_there_ref)[:: 1 if value == 0 else -1])

    return call(
        body,
        "turn",
        [SMEM] + [VM] * 4,
        shape((12, 192, 96), f32),
        (at, far_own, far_there, near_own, near_there),
        us=4,
    )


def sync(*values):
    return lax.optimization_barrier(values)


def add_low(a, b):
    return (a.astype(f32) + b.astype(f32)).astype(bf16)


def step_small(
    patches,
    cotangent,
    input_views,
    token_live,
    master,
    moment_one,
    moment_two,
    norm_params,
    norm_moment_one,
    norm_moment_two,
):
    tokens = patches.shape[0]
    rows, blocks, cols = master.shape
    dp = lax.axis_index("dp")
    seq = lax.axis_index("seq")
    quarter, x_place = seq // 2, seq % 2
    y_place, core = dp // 2, dp % 2
    place = gray(quarter)
    at = jnp.stack([x_place, y_place, core, place]).astype(jnp.int32)

    def to_core(value):
        return swap(value, "dp", 1)

    def to_y(value):
        return swap(value, "dp", 2)

    def to_x(value):
        return swap(value, "seq", 1)

    def by_core(first, second):
        return jnp.where(core == 0, first, second), jnp.where(core == 0, second, first)

    def by_y(first, second):
        return jnp.where(y_place == 0, first, second), jnp.where(y_place == 0, second, first)

    def own_y(value):
        return lax.dynamic_slice_in_dim(value, y_place * 384, 384, value.ndim - 1)

    def other_y(value):
        return lax.dynamic_slice_in_dim(value, (1 - y_place) * 384, 384, value.ndim - 1)

    master_t = jnp.transpose(master, (1, 0, 2))
    low_t = jnp.transpose(master_t.astype(bf16), (0, 2, 1))
    flags = jnp.pad(token_live.astype(bf16)[None, :], ((0, 7), (0, D - tokens)))
    out_block = jnp.pad(low_t[3], ((0, 0), (0, 256 - rows))).reshape(3, 32, 256)
    out_block = jnp.transpose(out_block, (1, 0, 2)).reshape(32, D)
    ring0 = jnp.concatenate([patches, flags, out_block], axis=0)
    near_halves = [low_t[0:3, h * HALF : (h + 1) * HALF].reshape(3 * HALF, rows) for h in range(2)]
    far_halves = [
        jnp.concatenate(
            [low_t[4 + 2 * h : 6 + 2 * h].reshape(2 * cols, rows), low_t[8 + 2 * h : 10 + 2 * h].reshape(2 * cols, rows)],
            axis=0,
        )
        for h in range(2)
    ]

    ring1, beside0 = hop_quarter(ring0, 1), to_x(ring0)
    own, other = by_core(*near_halves)
    near = jnp.concatenate(by_core(own, to_core(other)), axis=1)
    near = jnp.stack([near, to_x(near)])
    own, other = by_y(*far_halves)
    far0 = jnp.concatenate(by_y(own, to_y(other)), axis=1)
    ring1, beside0, near, far0 = sync(ring1, beside0, near, far0)

    ring2, beside1 = hop_quarter(ring1, 1), to_x(ring1)
    near = jnp.stack([near, to_y(near)])
    near_there = to_core(near)
    ring2, beside1, near, near_there = sync(ring2, beside1, near, near_there)

    ring3, beside2, cot_there = hop_quarter(ring2, 1), to_x(ring2), to_y(cotangent)
    w_qkv = place_qkv(at, near, near_there)
    got0 = list(project(ring0, beside0, w_qkv, norm_params))
    ring3, beside2, cot_there, first = sync(ring3, beside2, cot_there, got0[0])
    got0[0] = first

    beside3, far1 = to_x(ring3), hop_quarter(far0, 1)
    got1 = list(project(ring1, after(beside1, first), w_qkv, norm_params))
    got2 = list(project(ring2, beside2, w_qkv, norm_params))
    beside3, far1, got1[0], got2[0] = sync(beside3, far1, got1[0], got2[0])

    far2, far3 = hop_quarter(after(far1, beside3), 1), hop_quarter(after(far0, beside3), 3)
    far01 = jnp.stack([far0, far1])
    far01 = jnp.stack([far01, to_x(after(far01, beside3))], axis=1).reshape(4, 384, 384)
    out_own = jnp.stack([p[264:] for p in (ring0, beside0, ring1, beside1, ring2, beside2, ring3, beside3)])
    out_own = jnp.transpose(out_own.reshape(8, 32, 3, 256), (0, 2, 1, 3)).reshape(8, 96, 256)
    out_own = jnp.stack([out_own, to_y(out_own)])
    got3 = project(ring3, beside3, w_qkv, norm_params)
    acts, normals, qs, ks, vs = zip(got0, got1, got2, got3)
    mixed, full, q_back = attend(at, qs, ks, vs)
    mixed = list(mixed)
    *mixed, full, far2, far3, far01, out_own = sync(*mixed, full, far2, far3, far01, out_own)

    mixed = [mixed[0]] + [hop_quarter(mixed[4 - k], k) for k in (3, 2, 1)]
    far23 = jnp.stack([far2, far3])
    far23 = jnp.stack([far23, to_x(far23)], axis=1).reshape(4, 384, 384)
    w_out = place_out(at, out_own, to_core(out_own))
    *mixed, far23, w_out = sync(*mixed, far23, w_out)

    far01_there, far23_there = to_core(far01), to_core(far23)
    two, resid, normal_two, inverse_two, act_three = out_norm(at, patches, mixed, w_out, norm_params)
    w_mlp = (far01, far23, far01_there, far23_there)
    act_three, *w_mlp = sync(act_three, *w_mlp)

    act_there = to_y(act_three)
    hidden, wide, out_mine, three_mine = mlp(at, act_three, cotangent, w_mlp, f32)
    act_there, out_mine = sync(act_there, out_mine)
    hidden_there, wide_there, out_send, three_send = mlp(at, act_there, cot_there, w_mlp, bf16)
    three_send, hidden_there = sync(three_send, hidden_there)
    three_there = to_y(three_send)
    operands = (at, (act_three, act_there), (cotangent, cot_there), (hidden, hidden_there), (wide, wide_there))
    low_keep, low_send = mlp_weights(*operands, (1, 2))
    low_there = to_core(low_send)
    high_keep, high_send = mlp_weights(*operands, (3, 0))
    three_there, low_there, high_send = sync(three_there, low_there, high_send)

    low_sum = add_low(low_keep, low_there)
    low_x = to_x(low_sum[1])
    high_there = to_core(high_send)
    grad_resid, sums_two, parts, w_out_keep, w_out_send = norm_out_back(
        at, three_mine, three_there, cotangent, normal_two, inverse_two, two, w_out, norm_params
    )
    *parts, w_out_send, high_there = sync(*parts, w_out_send, high_there)

    grads = [parts[0]] + [hop_quarter(parts[k], k) for k in (1, 2, 3)]
    high_sum = add_low(high_keep, high_there)
    out_sum = add_low(w_out_keep, to_core(w_out_send))
    out_sum = add_low(own_y(out_sum), to_y(other_y(out_sum))).reshape(4, 2, HALF, 384)
    *grads, low_x, high_sum, out_sum = sync(*grads, low_x, high_sum, out_sum)

    low_half = add_low(low_sum[0], low_x)
    far_got = [hop_quarter(low_half[0], -1), hop_quarter(low_half[1], -2)]
    high_half = add_low(high_sum[0], to_x(high_sum[1]))
    out_sum = add_low(out_sum[:, 0], to_x(out_sum[:, 1]))
    dqs, dks, dvs = attend_back(at, q_back, ks, vs, full, grads)
    dqs = list(dqs)
    dqs[1], high_half, out_sum = sync(dqs[1], high_half, out_sum)

    last = hop_quarter(jnp.concatenate([high_half[0], out_sum[3]], axis=0), -3)
    out_got = [hop_quarter(out_sum[1], -1), hop_quarter(out_sum[2], -2), last[384:]]
    far_got = [*far_got, last[:384]]
    one, sums_one = {}, []
    for ks_here in ((1, 2), (3, 0)):
        keep, send, sums = input_back(*([m[k] for k in ks_here] for m in (normals, dqs, dks, dvs)), w_qkv)
        dqs[0], dqs[3] = after(dqs[0], keep[0]), after(dqs[3], keep[0])
        sums_one.append(sums)
        for k, a, b in zip(ks_here, keep, send):
            one[k] = (a, b)
    near_keep, near_send = projections_back(at, acts, dqs, dks, dvs)
    one1 = to_x(one[1][1])
    one2 = to_x(after(one[2][1], one[0][0]))
    out_there = to_y(after(out_send, near_keep))
    block_out = (resid + out_mine + out_there.astype(f32)).astype(bf16)
    one1, near_send, *far_got = sync(one1, near_send, *far_got)
    far_sum = high_half[1].astype(f32)
    for part in far_got:
        far_sum = far_sum + part.astype(f32)
    out_sum = out_sum[0].astype(f32)
    for part in out_got:
        out_sum = out_sum + part.astype(f32)

    one_ring = hop_quarter(add_low(one[1][0], one1), 1)
    one_ring = hop_quarter(add_low(one_ring, add_low(one[2][0], one2)), 1)
    near_sum = add_low(near_keep, to_core(near_send))
    near_sum = add_low(own_y(near_sum), to_y(other_y(near_sum)))
    near_x = to_x(near_sum[3:6])
    one3 = add_low(one[3][0], to_x(after(one[3][1], near_x)))
    one0 = add_low(one[0][0], to_x(after(one[0][1], near_x)))
    one_ring = hop_quarter(add_low(one_ring, one3), 1)
    grad_one = one_ring.astype(f32) + one0.astype(f32)
    normal_one, inverse_one = layer_stats(patches.astype(f32))
    patches_grad = grad_resid + layer_back(grad_one, normal_one, inverse_one, norm_params[0])
    param_grad = jnp.concatenate([sums_one[0][0:2] + sums_one[1][0:2], sums_two[0:2]], axis=0)

    near_sum = near_sum[0:3].astype(f32) + near_x.astype(f32)
    near_sum = jnp.concatenate([near_sum.reshape(3 * HALF, 2 * rows), out_sum], axis=0)
    far_own, far_other = by_y(far_sum[:, :rows], far_sum[:, rows:])
    near_own, near_other = by_core(near_sum[:, :rows], near_sum[:, rows:])
    weight_grad = turn(at, far_own, to_y(far_other.astype(bf16)), near_own, to_core(near_other.astype(bf16)))
    squares = jnp.full((4, D), jnp.sum(far_sum * far_sum) + jnp.sum(near_sum * near_sum), f32)
    sums = jnp.concatenate([param_grad, squares], axis=0)
    for by in (1, 2):
        sums = sums + hop_quarter(sums, by)
    sums = sums + swap(sums, "seq", 1)
    sums = after(sums, weight_grad)
    sums = sums + swap(sums, "dp", 2)
    sums = sums + swap(sums, "dp", 1)
    param_grad = sums[0:4]
    squares = sums[4, 0] + jnp.sum(param_grad * param_grad)
    grad_norm = jnp.sqrt(squares)
    clip = 1.0 / jnp.maximum(grad_norm, 1.0)
    moments = jnp.transpose(moment_one, (1, 0, 2)), jnp.transpose(moment_two, (1, 0, 2))
    new_master, *moments = adam_step(master_t, weight_grad * clip, *moments, rate_matrix, weight_decay)
    new_master, new_copy, new_moment_one, new_moment_two = (
        jnp.transpose(m, (1, 0, 2)) for m in (new_master, new_master.astype(bf16), *moments)
    )
    new_norm_params, new_norm_moment_one, new_norm_moment_two = adam_step(
        norm_params, param_grad * clip, norm_moment_one, norm_moment_two, rate_vector, 0.0
    )
    return (
        block_out,
        patches_grad,
        new_master,
        new_copy,
        new_moment_one,
        new_moment_two,
        new_norm_params,
        new_norm_moment_one,
        new_norm_moment_two,
        grad_norm,
    )


def solution(mesh):
    tokens = P(("dp", "seq"), None)
    weights = P("dp", None, "seq")
    small = mesh.shape["dp"] == 4 and mesh.shape["seq"] == 8
    return jax.shard_map(
        step_small if small else step_general,
        mesh=mesh,
        in_specs=(tokens, tokens, P("dp"), P(("dp", "seq")), weights, weights, weights, P(), P(), P()),
        out_specs=(tokens, tokens, weights, weights, weights, weights, P(), P(), P(), P()),
        check_vma=False,
    )
```

profile of v0, /device:TPU:0, one launch (start us, length us, event | category | flops | bytes accessed | tf_op | source)
XLA Modules:
  0.0 294.1 jit_solution(16312652504295079874)
XLA Ops:
  3.0 3.1 %collective-permute-start = (bf16[296,768]{1,0:T(8,128)(2,1)S(1)}, bf16[296,768]{1,0:T(8,128)(2,1)S(1)}, u32[]{:S(2)}, u32[]{:S(2)}) collective-permute-start(bf16[296,768]{1,0:T(8,128)(2,1)S(1)} %fusion.20.a_ref), channel_id=1, source_target_pairs={{0,2},{1,3},{2,6},{3,7},{6,4},{7,5},{4,0},{5,1},{8,10},{9,11},{10,... | collective-permute-start | bytes 1363976 | tf_op jit(solution)/shard_map/ppermute | solution.py:44
  10.8 4.8 %collective-permute-done.4 = bf16[384,192]{1,0:T(8,128)(2,1)S(1)} collective-permute-done((bf16[384,192]{1,0:T(8,128)(2,1)S(1)}, bf16[384,192]{1,0:T(8,128)(2,1)S(1)}, u32[]{:S(2)}, u32[]{:S(2)}) %collective-permute-start.4) | collective-permute-done | bytes 147488 | tf_op jit(solution)/shard_map/ppermute | solution.py:54
  15.8 4.5 %collective-permute-done.3 = bf16[144,384]{1,0:T(8,128)(2,1)S(1)} collective-permute-done((bf16[144,384]{1,0:T(8,128)(2,1)S(1)}, bf16[144,384]{1,0:T(8,128)(2,1)S(1)}, u32[]{:S(2)}, u32[]{:S(2)}) %collective-permute-start.3) | collective-permute-done | bytes 110624 | tf_op jit(solution)/shard_map/ppermute | solution.py:54
  28.5 8.5 %collective-permute-done.5.a_ref = bf16[296,768]{1,0:T(8,128)(2,1)} collective-permute-done((bf16[296,768]{1,0:T(8,128)(2,1)S(1)}, bf16[296,768]{1,0:T(8,128)(2,1)}, u32[]{:S(2)}, u32[]{:S(2)}) %collective-permute-start.5) | collective-permute-done | bytes 454688 | tf_op jit(solution)/shard_map/ppermute | solution.py:44
  42.8 2.9 %place_qkv.1.w_ref.refs_8_ = bf16[576,768]{1,0:T(8,128)(2,1)} custom-call(s32[4]{0:T(128)} %pad_add_fusion.at_ref, bf16[2,2,144,384]{3,2,1,0:T(8,128)(2,1)} %copy-done.16, bf16[2,2,144,384]{3,2,1,0:T(8,128)(2,1)} %copy-done.34), custom_call_target="tpu_custom_call" | custom-call | flops 4000000000 | bytes 14400000 | tf_op jit(solution)/shard_map/place_qkv/pallas_call | solution.py:362
  45.7 4.3 %norm_project.4 = (bf16[512,768]{1,0:T(8,128)(2,1)}, bf16[512,768]{1,0:T(8,128)(2,1)}, bf16[3,256,128]{2,1,0:T(8,128)(2,1)}, bf16[3,512,128]{2,1,0:T(8,128)(2,1)}, bf16[3,512,128]{2,1,0:T(8,128)(2,1)}) custom-call(bf16[296,768]{1,0:T(8,128)(2,1)} %copy-done.15, bf16[296,768]{1,0:T(8,128)(2,1)} %copy-done.29, bf16[576,768]{1,0:T(8,128)(2,1)} %place_qkv.1.w_ref.refs_8_, ...), custom_call_target="tpu_custom_call" | custom-call | flops 4000000000 | bytes 14400000 | tf_op jit(solution)/shard_map/norm_project/pallas_call | solution.py:362
  50.6 4.4 %norm_project.5 = (bf16[512,768]{1,0:T(8,128)(2,1)}, bf16[512,768]{1,0:T(8,128)(2,1)}, bf16[3,256,128]{2,1,0:T(8,128)(2,1)}, bf16[3,512,128]{2,1,0:T(8,128)(2,1)}, bf16[3,512,128]{2,1,0:T(8,128)(2,1)}) custom-call(bf16[296,768]{1,0:T(8,128)(2,1)} %copy-done.28, bf16[296,768]{1,0:T(8,128)(2,1)} %copy-done.30, bf16[576,768]{1,0:T(8,128)(2,1)} %place_qkv.1.w_ref.refs_8_, ...), custom_call_target="tpu_custom_call" | custom-call | flops 4000000000 | bytes 14400000 | tf_op jit(solution)/shard_map/norm_project/pallas_call | solution.py:362
  56.5 4.3 %norm_project.6 = (bf16[512,768]{1,0:T(8,128)(2,1)}, bf16[512,768]{1,0:T(8,128)(2,1)}, bf16[3,256,128]{2,1,0:T(8,128)(2,1)}, bf16[3,512,128]{2,1,0:T(8,128)(2,1)}, bf16[3,512,128]{2,1,0:T(8,128)(2,1)}) custom-call(bf16[296,768]{1,0:T(8,128)(2,1)} %collective-permute-done.5.a_ref, bf16[296,768]{1,0:T(8,128)(2,1)} %copy-done.22, ...), custom_call_target="tpu_custom_call" | custom-call | flops 4000000000 | bytes 14400000 | tf_op jit(solution)/shard_map/norm_project/pallas_call | solution.py:362
  61.7 3.4 %collective-permute-done.12.b_ref = bf16[296,768]{1,0:T(8,128)(2,1)S(1)} collective-permute-done((bf16[296,768]{1,0:T(8,128)(2,1)}, bf16[296,768]{1,0:T(8,128)(2,1)S(1)}, u32[]{:S(2)}, u32[]{:S(2)}) %collective-permute-start.12) | collective-permute-done | bytes 454688 | tf_op jit(solution)/shard_map/ppermute | solution.py:54
  65.9 4.3 %norm_project.7 = (bf16[512,768]{1,0:T(8,128)(2,1)}, bf16[512,768]{1,0:T(8,128)(2,1)}, bf16[3,256,128]{2,1,0:T(8,128)(2,1)}, bf16[3,512,128]{2,1,0:T(8,128)(2,1)}, bf16[3,512,128]{2,1,0:T(8,128)(2,1)}) custom-call(bf16[296,768]{1,0:T(8,128)(2,1)} %collective-permute-done.9.a_ref, bf16[296,768]{1,0:T(8,128)(2,1)} %copy-done.21, ...), custom_call_target="tpu_custom_call" | custom-call | flops 4000000000 | bytes 14400000 | tf_op jit(solution)/shard_map/norm_project/pallas_call | solution.py:362
  75.6 12.9 %attend.1 = (bf16[256,192]{1,0:T(8,128)(2,1)}, bf16[256,192]{1,0:T(8,128)(2,1)}, bf16[256,192]{1,0:T(8,128)(2,1)}, bf16[256,192]{1,0:T(8,128)(2,1)}, f32[4,3,256...) custom-call(s32[4]{0:T(128)} %pad_add_fusion.at_ref, bf16[3,256,128]{2,1,0:T(8,128)(2,1)} %get-tuple-element.167.refs_0_, ...), custom_call_target="tpu_custom_call" | custom-call | flops 12000000000 | bytes 43200000 | tf_op jit(solution)/shard_map/attend/pallas_call | solution.py:362
  90.4 2.9 %collective-permute-start.19 = (bf16[256,192]{1,0:T(8,128)(2,1)S(1)}, bf16[256,192]{1,0:T(8,128)(2,1)S(1)}, u32[]{:S(2)}, u32[]{:S(2)}) collective-permute-start(bf16[256,192]{1,0:T(8,128)(2,1)S(1)} %copy-done.49), channel_id=1, source_target_pairs={{0,6},{1,7},{2,4},{3,5},{6,0},{7,1},{4,2},{5,3},{8,14},{9,15},{10,... | collective-permute-start | bytes 294920 | tf_op jit(solution)/shard_map/ppermute | solution.py:44
  93.8 11.6 %collective-permute-done.21 = bf16[2,384,384]{2,1,0:T(8,128)(2,1)S(1)} collective-permute-done((bf16[2,384,384]{2,1,0:T(8,128)(2,1)S(1)}, bf16[2,384,384]{2,1,0:T(8,128)(2,1)S(1)}, u32[]{:S(2)}, u32[]{:S(2)}) %collective-permute-start.21) | collective-permute-done | bytes 589856 | tf_op jit(solution)/shard_map/ppermute | solution.py:54
  106.6 3.5 %place_out.1.w_ref = bf16[4,768,256]{2,1,0:T(8,128)(2,1)} custom-call(s32[4]{0:T(128)} %pad_add_fusion.at_ref, bf16[2,8,96,256]{3,2,1,0:T(8,128)(2,1)} %copy-done.10, bf16[2,8,96,256]{3,2,1,0:T(8,128)(2,1)} %copy-done.33), custom_call_target="tpu_custom_call" | custom-call | flops 3000000000 | bytes 10800000 | tf_op jit(solution)/shard_map/place_out/pallas_call | solution.py:362
  110.8 3.7 %out_norm.1 = (bf16[256,768]{1,0:T(8,128)(2,1)}, f32[256,768]{1,0:T(8,128)}, f32[256,768]{1,0:T(8,128)}, f32[256,128]{1,0:T(8,128)}, bf16[256,768]{1,0:T(8,128)(2,1)}) custom-call(s32[4]{0:T(128)} %pad_add_fusion.at_ref, bf16[256,768]{1,0:T(8,128)(2,1)} %x_ref.1, bf16[256,192]{1,0:T(8,128)(2,1)} %get-tuple-element.206.m0, bf16[256,192]{1,0:T(8,128)(2,1)} %copy-done.51, ...), custom_call_target="tpu_custom_call" | custom-call | flops 4000000000 | bytes 14400000 | tf_op jit(solution)/shard_map/out_norm/pallas_call | solution.py:362
  116.2 8.1 %mlp.2 = (bf16[256,1536]{1,0:T(8,128)(2,1)}, bf16[256,1536]{1,0:T(8,128)(2,1)}, f32[256,768]{1,0:T(8,128)}, f32[256,768]{1,0:T(8,128)}) custom-call(s32[4]{0:T(128)} %pad_add_fusion.at_ref, bf16[256,768]{1,0:T(8,128)(2,1)} %get-tuple-element.215.a_ref.refs_0_, bf16[256,768]{1,0:T(8,128)(2,1)} %c_ref.3, bf16[4,384,384]{2,1,0:T(8,128)(2,1)} %bitcast.129, ...), custom_call_target="tpu_custom_call" | custom-call | flops 8000000000 | bytes 28800000 | tf_op jit(solution)/shard_map/mlp/pallas_call | solution.py:362
  127.2 8.0 %mlp.3 = (bf16[256,1536]{1,0:T(8,128)(2,1)}, bf16[256,1536]{1,0:T(8,128)(2,1)}, bf16[256,768]{1,0:T(8,128)(2,1)}, bf16[256,768]{1,0:T(8,128)(2,1)}) custom-call(s32[4]{0:T(128)} %pad_add_fusion.at_ref, bf16[256,768]{1,0:T(8,128)(2,1)} %copy-done.39, bf16[256,768]{1,0:T(8,128)(2,1)} %collective-permute-done.11.c_ref.refs_3_, bf16[4,384,384]{2,1,0:T(8,128)(2,1)} %bitcast.130, ...), custom_call_target="tpu_custom_call" | custom-call | flops 8000000000 | bytes 28800000 | tf_op jit(solution)/shard_map/mlp/pallas_call | solution.py:362
  135.2 5.4 %mlp_weights.2 = (bf16[2,2,384,384]{3,2,1,0:T(8,128)(2,1)}, bf16[2,2,384,384]{3,2,1,0:T(8,128)(2,1)}) custom-call(s32[4]{0:T(128)} %pad_add_fusion.at_ref, bf16[256,768]{1,0:T(8,128)(2,1)} %get-tuple-element.215.a_ref.refs_0_, bf16[256,768]{1,0:T(8,128)(2,1)} %copy-done.39, bf16[256,768]{1,0:T(8,128)(2,1)} %c_ref.3, ...), custom_call_target="tpu_custom_call" | custom-call | flops 4000000000 | bytes 14400000 | tf_op jit(solution)/shard_map/mlp_weights/pallas_call | solution.py:362
  142.3 5.3 %mlp_weights.3 = (bf16[2,2,384,384]{3,2,1,0:T(8,128)(2,1)}, bf16[2,2,384,384]{3,2,1,0:T(8,128)(2,1)}) custom-call(s32[4]{0:T(128)} %pad_add_fusion.at_ref, bf16[256,768]{1,0:T(8,128)(2,1)} %get-tuple-element.215.a_ref.refs_0_, bf16[256,768]{1,0:T(8,128)(2,1)} %copy-done.39, bf16[256,768]{1,0:T(8,128)(2,1)} %c_ref.3, ...), custom_call_target="tpu_custom_call" | custom-call | flops 4000000000 | bytes 14400000 | tf_op jit(solution)/shard_map/mlp_weights/pallas_call | solution.py:362
  147.6 4.6 %collective-permute-done.26.s_ref = bf16[256,768]{1,0:T(8,128)(2,1)S(1)} collective-permute-done((bf16[256,768]{1,0:T(8,128)(2,1)S(1)}, bf16[256,768]{1,0:T(8,128)(2,1)S(1)}, u32[]{:S(2)}, u32[]{:S(2)}) %collective-permute-start.26) | collective-permute-done | bytes 393248 | tf_op jit(solution)/shard_map/ppermute | solution.py:54
  152.5 8.8 %fusion.15 = f32[256]{0:T(256)S(1)} fusion(bf16[256,768]{1,0:T(8,128)(2,1)S(1)} %copy-done.1, f32[256]{0:T(256)S(1)} %broadcast_multiply_fusion.2), kind=kLoop, calls=%fused_computation.31 | loop fusion | flops 786176 | bytes 395264 | tf_op jit(solution)/shard_map/reduce_sum | solution.py:75
  161.9 5.4 %norm_out_back.1 = (f32[256,768]{1,0:T(8,128)}, f32[8,768]{1,0:T(8,128)}, bf16[256,192]{1,0:T(8,128)(2,1)}, bf16[256,192]{1,0:T(8,128)(2,1)}, bf16[256,192]{1,0:...) custom-call(s32[4]{0:T(128)} %pad_add_fusion.at_ref, ...), custom_call_target="tpu_custom_call" | custom-call | flops 4000000000 | bytes 14400000 | tf_op jit(solution)/shard_map/norm_out_back/pallas_call | solution.py:362
  177.4 6.0 %collective-permute-done.34 = bf16[8,48,384]{2,1,0:T(8,128)(2,1)S(1)} collective-permute-done((bf16[8,48,384]{2,1,0:T(8,128)(2,1)S(1)}, bf16[8,48,384]{2,1,0:T(8,128)(2,1)S(1)}, u32[]{:S(2)}, u32[]{:S(2)}) %collective-permute-start.34) | collective-permute-done | bytes 294944 | tf_op jit(solution)/shard_map/ppermute | solution.py:54
  190.8 18.7 %attend_back.1 = (bf16[256,192]{1,0:T(8,128)(2,1)}, bf16[256,192]{1,0:T(8,128)(2,1)}, bf16[256,192]{1,0:T(8,128)(2,1)}, bf16[256,192]{1,0:T(8,128)(2,1)}, bf16[5...) custom-call(s32[4]{0:T(128)} %pad_add_fusion.at_ref, ...), custom_call_target="tpu_custom_call" | custom-call | flops 16000000000 | bytes 57600000 | tf_op jit(solution)/shard_map/attend_back/pallas_call | solution.py:362
  209.7 4.3 %input_back.2 = (bf16[256,768]{1,0:T(8,128)(2,1)}, bf16[256,768]{1,0:T(8,128)(2,1)}, bf16[256,768]{1,0:T(8,128)(2,1)}, bf16[256,768]{1,0:T(8,128)(2,1)}, f32[8,768]{1,0:T(8,128)}) custom-call(bf16[512,768]{1,0:T(8,128)(2,1)} %get-tuple-element.265.refs_0_, bf16[512,768]{1,0:T(8,128)(2,1)} %get-tuple-element.266.refs_1_, ...), custom_call_target="tpu_custom_call" | custom-call | flops 3000000000 | bytes 10800000 | tf_op jit(solution)/shard_map/input_back/pallas_call | solution.py:362
  214.0 4.3 %input_back.3 = (bf16[256,768]{1,0:T(8,128)(2,1)}, bf16[256,768]{1,0:T(8,128)(2,1)}, bf16[256,768]{1,0:T(8,128)(2,1)}, bf16[256,768]{1,0:T(8,128)(2,1)}, f32[8,768]{1,0:T(8,128)}) custom-call(bf16[512,768]{1,0:T(8,128)(2,1)} %get-tuple-element.278.refs_0_, bf16[512,768]{1,0:T(8,128)(2,1)} %get-tuple-element.279.refs_1_, ...), custom_call_target="tpu_custom_call" | custom-call | flops 3000000000 | bytes 10800000 | tf_op jit(solution)/shard_map/input_back/pallas_call | solution.py:362
  222.8 5.5 %projections_back.1 = (bf16[6,48,768]{2,1,0:T(8,128)(2,1)}, bf16[6,48,768]{2,1,0:T(8,128)(2,1)}) custom-call(s32[4]{0:T(128)} %pad_add_fusion.at_ref, bf16[512,768]{1,0:T(8,128)(2,1)} %get-tuple-element.171.refs_0_, bf16[512,768]{1,0:T(8,128)(2,1)} %get-tuple-element.225.refs_1_, bf16[512,768]{1,0:T(8,128)(2,1)} %get-tuple-element.226.refs_2_, ...), custom_call_target="tpu_custom_call" | custom-call | flops 6000000000 | bytes 21600000 | tf_op jit(solution)/shard_map/projections_back/pallas_call | solution.py:362
  238.6 5.0 %collective-permute-done.46 = bf16[6,48,384]{2,1,0:T(8,128)(2,1)S(1)} collective-permute-done((bf16[6,48,384]{2,1,0:T(8,128)(2,1)S(1)}, bf16[6,48,384]{2,1,0:T(8,128)(2,1)S(1)}, u32[]{:S(2)}, u32[]{:S(2)}) %collective-permute-start.46) | collective-permute-done | bytes 221216 | tf_op jit(solution)/shard_map/ppermute | solution.py:54
  252.1 4.0 %collective-permute-done.55 = f32[8,768]{1,0:T(8,128)S(1)} collective-permute-done((f32[8,768]{1,0:T(8,128)S(1)}, f32[8,768]{1,0:T(8,128)S(1)}, u32[]{:S(2)}, u32[]{:S(2)}) %collective-permute-start.55) | collective-permute-done | bytes 24608 | tf_op jit(solution)/shard_map/ppermute | solution.py:44
  256.1 2.6 collective-permute-start.56
  280.2 5.3 %collective-permute-start.49 = (bf16[256,768]{1,0:T(8,128)(2,1)S(1)}, bf16[256,768]{1,0:T(8,128)(2,1)S(1)}, u32[]{:S(2)}, u32[]{:S(2)}) collective-permute-start(bf16[256,768]{1,0:T(8,128)(2,1)S(1)} %add_convert_fusion.5), channel_id=1, source_target_pairs={{0,2},{1,3},{2,6},{3,7},{6,4},{7,5},{4,0},{5,1},{8,10},{9,11},{10,... | collective-permute-start | bytes 1179656 | tf_op jit(solution)/shard_map/ppermute | solution.py:44
  285.5 4.6 %convert_bitcast_fusion = (bf16[192,12,96]{2,0,1:T(8,128)(2,1)}, f32[12,192,96]{2,1,0:T(8,128)}, f32[192,12,96]{2,0,1:T(8,128)}, f32[192,12,96]{2,0,1:T(8,128)}) fusion(f32[192,12,96]{2,0,1:T(8,128)S(1)} %copy-done.4, f32[12,192,96]{2,1,0:T(8,128)} %turn.1, f32[]{:T(128)S(6)} %div.70, f32[192,12,96]{2,0,1:T(8,128)} %param.14, f32[192,12,96]{2,0,1:T(8,128)S(1)} %copy-done.2), kind=kLoop, calls=%fused_computation.49 | loop fusion | flops 3760128 | bytes 6635524 | tf_op jit(solution)/shard_map/transpose | solution.py:1158
  (319 shorter events, 103.1 us)
Async XLA Ops:
  3.0 17.4 %collective-permute-start = (bf16[296,768]{1,0:T(8,128)(2,1)S(1)}, bf16[296,768]{1,0:T(8,128)(2,1)S(1)}, u32[]{:S(2)}, u32[]{:S(2)}) collective-permute-start(bf16[296,768]{1,0:T(8,128)(2,1)S(1)} %fusion.20.a_ref), channel_id=1, source_target_pairs={{0,2},{1,3},{2,6},{3,7},{6,4},{7,5},{4,0},{5,1},{8,10},{9,11},{10,... | collective-permute-start | bytes 1363976 | tf_op jit(solution)/shard_map/ppermute | solution.py:44
  6.1 14.3 %collective-permute-start.1 = (bf16[296,768]{1,0:T(8,128)(2,1)S(1)}, bf16[296,768]{1,0:T(8,128)(2,1)S(1)}, u32[]{:S(2)}, u32[]{:S(2)}) collective-permute-start(bf16[296,768]{1,0:T(8,128)(2,1)S(1)} %fusion.20.a_ref), channel_id=1, source_target_pairs={{0,1},{1,0},{2,3},{3,2},{4,5},{5,4},{6,7},{7,6},{8,9},{9,8},{10,11... | collective-permute-start | bytes 1363976 | tf_op jit(solution)/shard_map/ppermute | solution.py:54
  9.4 40.6 %collective-permute-start.11 = (bf16[256,768]{1,0:T(8,128)(2,1)}, bf16[256,768]{1,0:T(8,128)(2,1)}, u32[]{:S(2)}, u32[]{:S(2)}) collective-permute-start(bf16[256,768]{1,0:T(8,128)(2,1)} %c_ref.3), channel_id=1, source_target_pairs={{0,16},{8,24},{16,0},{24,8},{1,17},{9,25},{17,1},{25,9},{2,18},{10... | collective-permute-start | bytes 1179656 | tf_op jit(solution)/shard_map/ppermute | solution.py:54
  22.7 14.4 %collective-permute-start.5 = (bf16[296,768]{1,0:T(8,128)(2,1)S(1)}, bf16[296,768]{1,0:T(8,128)(2,1)}, u32[]{:S(2)}, u32[]{:S(2)}) collective-permute-start(bf16[296,768]{1,0:T(8,128)(2,1)S(1)} %collective-permute-done.a_ref), channel_id=1, source_target_pairs={{0,2},{1,3},{2,6},{3,7},{6,4},{7,5},{4,0},{5,1},{8,10},{9,11},{10,... | collective-permute-start | bytes 1363976 | tf_op jit(solution)/shard_map/ppermute | solution.py:44
  25.3 11.8 %collective-permute-start.6 = (bf16[296,768]{1,0:T(8,128)(2,1)S(1)}, bf16[296,768]{1,0:T(8,128)(2,1)S(1)}, u32[]{:S(2)}, u32[]{:S(2)}) collective-permute-start(bf16[296,768]{1,0:T(8,128)(2,1)S(1)} %collective-permute-done.a_ref), channel_id=1, source_target_pairs={{0,1},{1,0},{2,3},{3,2},{4,5},{5,4},{6,7},{7,6},{8,9},{9,8},{10,11... | collective-permute-start | bytes 1363976 | tf_op jit(solution)/shard_map/ppermute | solution.py:54
  26.8 34.9 %collective-permute-start.13 = (bf16[384,384]{1,0:T(8,128)(2,1)S(1)}, bf16[384,384]{1,0:T(8,128)(2,1)S(1)}, u32[]{:S(2)}, u32[]{:S(2)}) collective-permute-start(bf16[384,384]{1,0:T(8,128)(2,1)S(1)} %pad_maximum_fusion.8), channel_id=1, source_target_pairs={{0,2},{1,3},{2,6},{3,7},{6,4},{7,5},{4,0},{5,1},{8,10},{9,11},{10,... | collective-permute-start | bytes 884744 | tf_op jit(solution)/shard_map/ppermute | solution.py:44
  37.9 12.7 %collective-permute-start.9 = (bf16[296,768]{1,0:T(8,128)(2,1)}, bf16[296,768]{1,0:T(8,128)(2,1)}, u32[]{:S(2)}, u32[]{:S(2)}) collective-permute-start(bf16[296,768]{1,0:T(8,128)(2,1)} %collective-permute-done.5.a_ref), channel_id=1, source_target_pairs={{0,2},{1,3},{2,6},{3,7},{6,4},{7,5},{4,0},{5,1},{8,10},{9,11},{10,... | collective-permute-start | bytes 1363976 | tf_op jit(solution)/shard_map/ppermute | solution.py:44
  70.2 18.7 %collective-permute-start.14 = (bf16[384,384]{1,0:T(8,128)(2,1)S(1)}, bf16[384,384]{1,0:T(8,128)(2,1)S(1)}, u32[]{:S(2)}, u32[]{:S(2)}) collective-permute-start(bf16[384,384]{1,0:T(8,128)(2,1)S(1)} %collective-permute-done.13), channel_id=1, source_target_pairs={{0,2},{1,3},{2,6},{3,7},{6,4},{7,5},{4,0},{5,1},{8,10},{9,11},{10,... | collective-permute-start | bytes 884744 | tf_op jit(solution)/shard_map/ppermute | solution.py:44
  71.9 17.1 %collective-permute-start.15 = (bf16[384,384]{1,0:T(8,128)(2,1)S(1)}, bf16[384,384]{1,0:T(8,128)(2,1)S(1)}, u32[]{:S(2)}, u32[]{:S(2)}) collective-permute-start(bf16[384,384]{1,0:T(8,128)(2,1)S(1)} %pad_maximum_fusion.8), channel_id=1, source_target_pairs={{0,4},{1,5},{2,0},{3,1},{6,2},{7,3},{4,6},{5,7},{8,12},{9,13},{10,... | collective-permute-start | bytes 884744 | tf_op jit(solution)/shard_map/ppermute | solution.py:44
  73.4 15.2 %collective-permute-start.16 = (bf16[2,384,384]{2,1,0:T(8,128)(2,1)S(1)}, bf16[2,384,384]{2,1,0:T(8,128)(2,1)S(1)}, u32[]{:S(2)}, u32[]{:S(2)}) collective-permute-start(bf16[2,384,384]{2,1,0:T(8,128)(2,1)S(1)} %get-tuple-element.198), channel_id=1, source_target_pairs={{0,1},{1,0},{2,3},{3,2},{4,5},{5,4},{6,7},{7,6},{8,9},{9,8},{10,11... | collective-permute-start | bytes 1769480 | tf_op jit(solution)/shard_map/ppermute | solution.py:54
  75.0 13.4 %collective-permute-start.17 = (bf16[8,96,256]{2,1,0:T(8,128)(2,1)S(1)}, bf16[8,96,256]{2,1,0:T(8,128)(2,1)S(1)}, u32[]{:S(2)}, u32[]{:S(2)}) collective-permute-start(bf16[8,96,256]{2,1,0:T(8,128)(2,1)S(1)} %bitcast.146), channel_id=1, source_target_pairs={{0,16},{8,24},{16,0},{24,8},{1,17},{9,25},{17,1},{25,9},{2,18},{10... | collective-permute-start | bytes 1179656 | tf_op jit(solution)/shard_map/ppermute | solution.py:54
  89.5 16.2 %collective-permute-start.22 = (bf16[2,8,96,256]{3,2,1,0:T(8,128)(2,1)S(1)}, bf16[2,8,96,256]{3,2,1,0:T(8,128)(2,1)S(1)}, u32[]{:S(2)}, u32[]{:S(2)}) collective-permute-start(bf16[2,8,96,256]{3,2,1,0:T(8,128)(2,1)S(1)} %pad_maximum_fusion.2.own_ref), channel_id=1, source_target_pairs={{0,8},{8,0},{16,24},{24,16},{1,9},{9,1},{17,25},{25,17},{2,10},{10... | collective-permute-start | bytes 2359304 | tf_op jit(solution)/shard_map/ppermute | solution.py:54
  89.6 15.8 %collective-permute-start.21 = (bf16[2,384,384]{2,1,0:T(8,128)(2,1)S(1)}, bf16[2,384,384]{2,1,0:T(8,128)(2,1)S(1)}, u32[]{:S(2)}, u32[]{:S(2)}) collective-permute-start(bf16[2,384,384]{2,1,0:T(8,128)(2,1)S(1)} %get-tuple-element.328), channel_id=1, source_target_pairs={{0,1},{1,0},{2,3},{3,2},{4,5},{5,4},{6,7},{7,6},{8,9},{9,8},{10,11... | collective-permute-start | bytes 1769480 | tf_op jit(solution)/shard_map/ppermute | solution.py:54
  90.2 19.9 %collective-permute-start.18 = (bf16[256,192]{1,0:T(8,128)(2,1)S(1)}, bf16[256,192]{1,0:T(8,128)(2,1)S(1)}, u32[]{:S(2)}, u32[]{:S(2)}) collective-permute-start(bf16[256,192]{1,0:T(8,128)(2,1)S(1)} %copy-done.50), channel_id=1, source_target_pairs={{0,4},{1,5},{2,0},{3,1},{6,2},{7,3},{4,6},{5,7},{8,12},{9,13},{10,... | collective-permute-start | bytes 294920 | tf_op jit(solution)/shard_map/ppermute | solution.py:44
  90.4 19.7 %collective-permute-start.19 = (bf16[256,192]{1,0:T(8,128)(2,1)S(1)}, bf16[256,192]{1,0:T(8,128)(2,1)S(1)}, u32[]{:S(2)}, u32[]{:S(2)}) collective-permute-start(bf16[256,192]{1,0:T(8,128)(2,1)S(1)} %copy-done.49), channel_id=1, source_target_pairs={{0,6},{1,7},{2,4},{3,5},{6,0},{7,1},{4,2},{5,3},{8,14},{9,15},{10,... | collective-permute-start | bytes 294920 | tf_op jit(solution)/shard_map/ppermute | solution.py:44
  93.3 16.8 %collective-permute-start.20 = (bf16[256,192]{1,0:T(8,128)(2,1)S(1)}, bf16[256,192]{1,0:T(8,128)(2,1)S(1)}, u32[]{:S(2)}, u32[]{:S(2)}) collective-permute-start(bf16[256,192]{1,0:T(8,128)(2,1)S(1)} %copy-done.48), channel_id=1, source_target_pairs={{0,2},{1,3},{2,6},{3,7},{6,4},{7,5},{4,0},{5,1},{8,10},{9,11},{10,... | collective-permute-start | bytes 294920 | tf_op jit(solution)/shard_map/ppermute | solution.py:44
  114.6 11.8 %collective-permute-start.25 = (bf16[256,768]{1,0:T(8,128)(2,1)}, bf16[256,768]{1,0:T(8,128)(2,1)S(1)}, u32[]{:S(2)}, u32[]{:S(2)}) collective-permute-start(bf16[256,768]{1,0:T(8,128)(2,1)} %get-tuple-element.215.a_ref.refs_0_), channel_id=1, source_target_pairs={{0,16},{8,24},{16,0},{24,8},{1,17},{9,25},{17,1},{25,9},{2,18},{10... | collective-permute-start | bytes 1179656 | tf_op jit(solution)/shard_map/ppermute | solution.py:54
  140.6 11.6 %collective-permute-start.27 = (bf16[2,2,384,384]{3,2,1,0:T(8,128)(2,1)}, bf16[2,2,384,384]{3,2,1,0:T(8,128)(2,1)S(1)}, u32[]{:S(2)}, u32[]{:S(2)}) collective-permute-start(bf16[2,2,384,384]{3,2,1,0:T(8,128)(2,1)} %get-tuple-element.238), channel_id=1, source_target_pairs={{0,8},{8,0},{16,24},{24,16},{1,9},{9,1},{17,25},{25,17},{2,10},{10... | collective-permute-start | bytes 3538952 | tf_op jit(solution)/shard_map/ppermute | solution.py:54
  152.2 15.0 %collective-permute-start.28 = (bf16[2,2,384,384]{3,2,1,0:T(8,128)(2,1)}, bf16[2,2,384,384]{3,2,1,0:T(8,128)(2,1)S(1)}, u32[]{:S(2)}, u32[]{:S(2)}) collective-permute-start(bf16[2,2,384,384]{3,2,1,0:T(8,128)(2,1)} %get-tuple-element.249), channel_id=1, source_target_pairs={{0,8},{8,0},{16,24},{24,16},{1,9},{9,1},{17,25},{25,17},{2,10},{10... | collective-permute-start | bytes 3538952 | tf_op jit(solution)/shard_map/ppermute | solution.py:54
  169.5 15.3 %collective-permute-start.32 = (bf16[2,384,384]{2,1,0:T(8,128)(2,1)S(1)}, bf16[2,384,384]{2,1,0:T(8,128)(2,1)S(1)}, u32[]{:S(2)}, u32[]{:S(2)}) collective-permute-start(bf16[2,384,384]{2,1,0:T(8,128)(2,1)S(1)} %slice_bitcast_fusion.1), channel_id=1, source_target_pairs={{0,1},{1,0},{2,3},{3,2},{4,5},{5,4},{6,7},{7,6},{8,9},{9,8},{10,11... | collective-permute-start | bytes 1769480 | tf_op jit(solution)/shard_map/ppermute | solution.py:54
  170.9 14.0 %collective-permute-start.29 = (bf16[256,192]{1,0:T(8,128)(2,1)S(1)}, bf16[256,192]{1,0:T(8,128)(2,1)S(1)}, u32[]{:S(2)}, u32[]{:S(2)}) collective-permute-start(bf16[256,192]{1,0:T(8,128)(2,1)S(1)} %copy-done.47), channel_id=1, source_target_pairs={{0,2},{1,3},{2,6},{3,7},{6,4},{7,5},{4,0},{5,1},{8,10},{9,11},{10,... | collective-permute-start | bytes 294920 | tf_op jit(solution)/shard_map/ppermute | solution.py:44
  171.7 13.2 %collective-permute-start.30 = (bf16[256,192]{1,0:T(8,128)(2,1)S(1)}, bf16[256,192]{1,0:T(8,128)(2,1)S(1)}, u32[]{:S(2)}, u32[]{:S(2)}) collective-permute-start(bf16[256,192]{1,0:T(8,128)(2,1)S(1)} %copy-done.45), channel_id=1, source_target_pairs={{0,6},{1,7},{2,4},{3,5},{6,0},{7,1},{4,2},{5,3},{8,14},{9,15},{10,... | collective-permute-start | bytes 294920 | tf_op jit(solution)/shard_map/ppermute | solution.py:44
  185.0 24.6 %collective-permute-start.35 = (bf16[2,384,384]{2,1,0:T(8,128)(2,1)S(1)}, bf16[2,384,384]{2,1,0:T(8,128)(2,1)S(1)}, u32[]{:S(2)}, u32[]{:S(2)}) collective-permute-start(bf16[2,384,384]{2,1,0:T(8,128)(2,1)S(1)} %slice_bitcast_fusion.2), channel_id=1, source_target_pairs={{0,1},{1,0},{2,3},{3,2},{4,5},{5,4},{6,7},{7,6},{8,9},{9,8},{10,11... | collective-permute-start | bytes 1769480 | tf_op jit(solution)/shard_map/ppermute | solution.py:54
  185.6 23.9 %collective-permute-start.36 = (bf16[4,48,384]{2,1,0:T(8,128)(2,1)S(1)}, bf16[4,48,384]{2,1,0:T(8,128)(2,1)S(1)}, u32[]{:S(2)}, u32[]{:S(2)}) collective-permute-start(bf16[4,48,384]{2,1,0:T(8,128)(2,1)S(1)} %slice_bitcast_fusion.6), channel_id=1, source_target_pairs={{0,1},{1,0},{2,3},{3,2},{4,5},{5,4},{6,7},{7,6},{8,9},{9,8},{10,11... | collective-permute-start | bytes 442376 | tf_op jit(solution)/shard_map/ppermute | solution.py:54
  187.4 46.4 %collective-permute-start.39 = (bf16[384,384]{1,0:T(8,128)(2,1)S(1)}, bf16[384,384]{1,0:T(8,128)(2,1)S(1)}, u32[]{:S(2)}, u32[]{:S(2)}) collective-permute-start(bf16[384,384]{1,0:T(8,128)(2,1)S(1)} %get-tuple-element.326), channel_id=1, source_target_pairs={{0,4},{1,5},{2,0},{3,1},{6,2},{7,3},{4,6},{5,7},{8,12},{9,13},{10,... | collective-permute-start | bytes 884744 | tf_op jit(solution)/shard_map/ppermute | solution.py:44
  189.5 44.3 %collective-permute-start.40 = (bf16[384,384]{1,0:T(8,128)(2,1)S(1)}, bf16[384,384]{1,0:T(8,128)(2,1)S(1)}, u32[]{:S(2)}, u32[]{:S(2)}) collective-permute-start(bf16[384,384]{1,0:T(8,128)(2,1)S(1)} %get-tuple-element.325), channel_id=1, source_target_pairs={{0,6},{1,7},{2,4},{3,5},{6,0},{7,1},{4,2},{5,3},{8,14},{9,15},{10,... | collective-permute-start | bytes 884744 | tf_op jit(solution)/shard_map/ppermute | solution.py:44
  218.3 15.5 %collective-permute-start.38 = (bf16[256,768]{1,0:T(8,128)(2,1)S(1)}, bf16[256,768]{1,0:T(8,128)(2,1)S(1)}, u32[]{:S(2)}, u32[]{:S(2)}) collective-permute-start(bf16[256,768]{1,0:T(8,128)(2,1)S(1)} %copy-done.37), channel_id=1, source_target_pairs={{0,1},{1,0},{2,3},{3,2},{4,5},{5,4},{6,7},{7,6},{8,9},{9,8},{10,11... | collective-permute-start | bytes 1179656 | tf_op jit(solution)/shard_map/ppermute | solution.py:54
  231.1 37.6 %collective-permute-start.43 = (bf16[256,768]{1,0:T(8,128)(2,1)S(1)}, bf16[256,768]{1,0:T(8,128)(2,1)S(1)}, u32[]{:S(2)}, u32[]{:S(2)}) collective-permute-start(bf16[256,768]{1,0:T(8,128)(2,1)S(1)} %copy-done.36), channel_id=1, source_target_pairs={{0,1},{1,0},{2,3},{3,2},{4,5},{5,4},{6,7},{7,6},{8,9},{9,8},{10,11... | collective-permute-start | bytes 1179656 | tf_op jit(solution)/shard_map/ppermute | solution.py:54
  244.5 24.2 %collective-permute-start.42 = (bf16[256,768]{1,0:T(8,128)(2,1)S(1)}, bf16[256,768]{1,0:T(8,128)(2,1)S(1)}, u32[]{:S(2)}, u32[]{:S(2)}) collective-permute-start(bf16[256,768]{1,0:T(8,128)(2,1)S(1)} %add_convert_fusion.9), channel_id=1, source_target_pairs={{0,2},{1,3},{2,6},{3,7},{6,4},{7,5},{4,0},{5,1},{8,10},{9,11},{10,... | collective-permute-start | bytes 1179656 | tf_op jit(solution)/shard_map/ppermute | solution.py:44
  245.6 17.7 %collective-permute-start.51 = (bf16[384,192]{1,0:T(8,128)(2,1)S(1)}, bf16[384,192]{1,0:T(8,128)(2,1)S(1)}, u32[]{:S(2)}, u32[]{:S(2)}) collective-permute-start(bf16[384,192]{1,0:T(8,128)(2,1)S(1)} %select_convert_fusion), channel_id=1, source_target_pairs={{0,16},{8,24},{16,0},{24,8},{1,17},{9,25},{17,1},{25,9},{2,18},{10... | collective-permute-start | bytes 442376 | tf_op jit(solution)/shard_map/ppermute | solution.py:54
  252.0 12.8 %collective-permute-start.54 = (bf16[192,192]{1,0:T(8,128)(2,1)S(1)}, bf16[192,192]{1,0:T(8,128)(2,1)S(1)}, u32[]{:S(2)}, u32[]{:S(2)}) collective-permute-start(bf16[192,192]{1,0:T(8,128)(2,1)S(1)} %select_convert_fusion.1), channel_id=1, source_target_pairs={{0,8},{8,0},{16,24},{24,16},{1,9},{9,1},{17,25},{25,17},{2,10},{10... | collective-permute-start | bytes 221192 | tf_op jit(solution)/shard_map/ppermute | solution.py:54
  272.9 17.1 %collective-permute-start.50 = (bf16[256,768]{1,0:T(8,128)(2,1)}, bf16[256,768]{1,0:T(8,128)(2,1)S(1)}, u32[]{:S(2)}, u32[]{:S(2)}) collective-permute-start(bf16[256,768]{1,0:T(8,128)(2,1)} %get-tuple-element.306), channel_id=1, source_target_pairs={{0,1},{1,0},{2,3},{3,2},{4,5},{5,4},{6,7},{7,6},{8,9},{9,8},{10,11... | collective-permute-start | bytes 1179656 | tf_op jit(solution)/shard_map/ppermute | solution.py:54
  (85 other events, 535.4 us)
where the time goes:
time: 299 us; the launch traced here: 294 us
  Pallas kernels  108 us (36%)
  waiting for transfers between devices  69.4 us (23%)
  starting transfers between devices  68.7 us (23%)
  other arithmetic  30.4 us (10%)
  local copies, waits for them, and re-layouts  11.8 us (4%)
  between operations  5.91 us (2%)
    pallas_call x18, Pallas kernels, call(): pl.pallas_call(body, name=name, out_shape=outs, in_specs=ins, out_specs=o...  108 us
    ppermute x38, waiting for transfers between devices, swap(): lax.ppermute(value, axis, [(i, i ^ bit) for i in range(lax.axis_size(axis...  48.4 us
    ppermute x22, starting transfers between devices, hop_quarter(): return lax.ppermute(value, 'seq', pairs)  36 us
    ppermute x38, starting transfers between devices, swap(): lax.ppermute(value, axis, [(i, i ^ bit) for i in range(lax.axis_size(axis...  32.7 us
    ppermute x22, waiting for transfers between devices, hop_quarter(): return lax.ppermute(value, 'seq', pairs)  21 us
    reduce_sum x1, other arithmetic, layer_stats(): spread = jnp.mean(shifted * shifted, axis=-1, keepdims=True)  8.77 us
    unnamed x118, local copies, waits for them, and re-layouts  6.36 us
  transfers between devices with their start and end apart: 60, of which 22 were waited for; matrix products, arithmetic and copies ran while one was open for 11% of the time, Pallas kernels for 31%

commit v1 on v0

--- a/solution.py
+++ b/solution.py
@@ -354,11 +354,11 @@
 HALF = 48
 ANY = pl.BlockSpec(memory_space=pl.ANY)
 SMEM = pl.BlockSpec(memory_space=pltpu.SMEM)
-VMEM_LIMIT = 56 << 20
-SCALE = 1.0
-
-
-def call(body, name, ins, outs, operands, scratch=(), us=4, out_specs=None, aliases=None):
+VMEM_LIMIT = 20
+SCALE = 0.1
+
+
+def call(body, name, ins, outs, operands, scratch=(), us=4, out_specs=None, aliases=None, mem=None):
     return pl.pallas_call(
         body,
         name=name,
@@ -368,7 +368,7 @@
         scratch_shapes=list(scratch),
         input_output_aliases=aliases or {},
         cost_estimate=pl.CostEstimate(flops=int(us * SCALE * 1e9), bytes_accessed=int(us * SCALE * 3.6e6), transcendentals=0),
-        compiler_params=pltpu.CompilerParams(vmem_limit_bytes=VMEM_LIMIT),
+        compiler_params=pltpu.CompilerParams(vmem_limit_bytes=(mem or VMEM_LIMIT) << 20),
     )(*operands)
 
 
@@ -459,7 +459,7 @@
 
 
 def project(first, second, w_t, norms):
-    def body(a_ref, b_ref, w_ref, norm_ref, act_ref, normal_ref, q_ref, k_ref, v_ref, wide_ref):
+    def body(a_ref, b_ref, w_ref, norm_ref, act_ref, normal_ref, q_ref, k_ref, v_ref, out_ref, wide_ref):
         wide_ref[...] = jnp.zeros_like(wide_ref)
         for h in range(9):
             wide_ref[h * 128 : h * 128 + 64, :] = w_ref[h * 64 : h * 64 + 64, :]
@@ -470,6 +470,8 @@
             act = (normal * gain + shift).astype(bf16)
             normal_ref[at, :] = normal.astype(bf16)
             act_ref[at, :] = act
+            for n in range(3):
+                out_ref[piece, n * 32 : n * 32 + 32, :] = ref[264:296, n * 256 : n * 256 + 256]
             flags = ref[256:257, 0:256].astype(f32)
             mask = jnp.where(flags > 0, 0.0, masked_score)
             mask = jnp.transpose(jnp.broadcast_to(mask, (128, 256)))
@@ -491,6 +493,7 @@
         shape((3, 256, 128), bf16),
         shape((3, 512, 128), bf16),
         shape((3, 512, 128), bf16),
+        shape((2, 96, 256), bf16),
     ]
     return call(body, "norm_project", [VM] * 4, outs, (first, second, w_t, norms), [pltpu.VMEM((1152, D), bf16)], us=4)
 
@@ -639,6 +642,7 @@
             pltpu.SemaphoreType.DMA((8,)),
         ],
         us=16,
+        mem=32,
     )
     return got[0:4], got[4:8], got[8:12]
 
@@ -753,7 +757,7 @@
                     for u in range(2):
                         group.append(
                             pltpu.make_async_copy(
-                                w_refs[2 * r + k // 2].at[2 * (k % 2) + j, pl.ds(u * 192, 192), :],
+                                w_refs[2 * r + (k == 2)].at[2 * (0, 1, 0, 2)[k] + j, pl.ds(u * 192, 192), :],
                                 w_ref.at[k, u, pl.ds(j * 192, 192), lanes],
                                 sems.at[k, len(group)],
                             )
@@ -858,11 +862,11 @@
     )
 
 
-def norm_out_back(at, three, three_there, cotangent, normal, inverse, two, w_out, norms):
-    def body(at_ref, t_ref, s_ref, c_ref, n_ref, i_ref, two_ref, w_ref, norm_ref, *outs):
+def norm_out_back(at, three, three_there, cotangent, normal, inverse, w_out, norms):
+    def body(at_ref, t_ref, s_ref, c_ref, n_ref, i_ref, w_ref, norm_ref, *outs):
         resid_ref, sums_ref = outs[0:2]
-        g_refs, keep_ref, send_ref, dw_ref = outs[2:6], outs[6], outs[7], outs[8]
-        x, c, place = at_ref[0], at_ref[2], at_ref[3]
+        g_refs, low_ref = outs[2:6], outs[6]
+        place = at_ref[3]
         grad = t_ref[...] + s_ref[...].astype(f32)
         normal = n_ref[...]
         sums_ref[...] = jnp.concatenate(
@@ -879,7 +883,26 @@
             for a in (1, 2, 3):
                 part = jnp.where(ahead == a, groups[a], part)
             g_refs[k][...] = part.astype(bf16)
-        dw_ref[...] = mm_tn(low, two_ref[...])
+        low_ref[...] = low
+
+    outs = (
+        [shape((256, D), f32), shape((8, D), f32)] + [shape((256, GROUP_WIDTH), bf16)] * 4 + [shape((256, D), bf16)]
+    )
+    got = call(
+        body,
+        "norm_out_back",
+        [SMEM] + [VM] * 7,
+        outs,
+        (at, three, three_there, cotangent, normal, inverse, w_out, norms),
+        us=4,
+    )
+    return got[0], got[1], got[2:6], got[6]
+
+
+def out_weights(at, low, two):
+    def body(at_ref, low_ref, two_ref, keep_ref, send_ref, dw_ref):
+        x, c, place = at_ref[0], at_ref[2], at_ref[3]
+        dw_ref[...] = mm_tn(low_ref[...], two_ref[...])
         for q in range(4):
             for xa in range(2):
                 slot = ((place - gray(q)) & 3) * 2 + (x ^ xa)
@@ -895,23 +918,15 @@
                     def _():
                         send_ref[slot] = block
 
-    outs = (
-        [shape((256, D), f32), shape((8, D), f32)]
-        + [shape((256, GROUP_WIDTH), bf16)] * 4
-        + [shape((8, HALF, D), bf16)] * 2
-    )
-    got = call(
+    return call(
         body,
-        "norm_out_back",
-        [SMEM] + [VM] * 8,
-        outs,
-        (at, three, three_there, cotangent, normal, inverse, two, w_out, norms),
+        "out_weights",
+        [SMEM, VM, VM],
+        [shape((8, HALF, D), bf16)] * 2,
+        (at, low, two),
         [pltpu.VMEM((D, D), f32)],
-    )
-    return got[0], got[1], got[2:6], got[6], got[7]
-
-
-FAR_AFTER = 3
+        us=3,
+    )
 
 
 def after(value, *others):
@@ -951,6 +966,31 @@
         (at, far_own, far_there, near_own, near_there),
         us=4,
     )
+
+
+def update(sums, weights, norms):
+    def body(sums_ref, w_ref, g_ref, first_ref, second_ref, p_ref, p_first_ref, p_second_ref, *outs):
+        grads = sums_ref[0:4, :]
+        total_squares = sums_ref[4:5, 0:1] + jnp.sum(jnp.sum(grads * grads, axis=1, keepdims=True), axis=0, keepdims=True)
+        norm = jnp.sqrt(total_squares)
+        outs[7][...] = jnp.broadcast_to(norm, (8, 128))
+        clip = 1.0 / jnp.maximum(norm, 1.0)
+        new = adam_step(p_ref[...], grads * clip, p_first_ref[...], p_second_ref[...], rate_vector, 0.0)
+        for ref, value in zip(outs[4:7], new):
+            ref[...] = value
+        for b in range(w_ref.shape[0]):
+            new, first, second = adam_step(
+                w_ref[b], g_ref[b] * clip, first_ref[b], second_ref[b], rate_matrix, weight_decay
+            )
+            outs[0][b] = new
+            outs[1][b] = new.astype(bf16)
+            outs[2][b] = first
+            outs[3][b] = second
+
+    dims = weights[0].shape
+    outs = [shape(dims, f32), shape(dims, bf16), shape(dims, f32), shape(dims, f32)]
+    outs = outs + [shape((4, D), f32)] * 3 + [shape((8, 128), f32)]
+    return call(body, "update", [VM] * 8, outs, (sums, *weights, *norms), us=4)
 
 
 def sync(*values):
@@ -1037,32 +1077,30 @@
     ring3, beside2, cot_there, first = sync(ring3, beside2, cot_there, got0[0])
     got0[0] = first
 
-    beside3, far1 = to_x(ring3), hop_quarter(far0, 1)
+    beside3, far1, far3 = to_x(ring3), hop_quarter(after(far0, ring3), 1), hop_quarter(after(far0, ring3), 3)
     got1 = list(project(ring1, after(beside1, first), w_qkv, norm_params))
     got2 = list(project(ring2, beside2, w_qkv, norm_params))
-    beside3, far1, got1[0], got2[0] = sync(beside3, far1, got1[0], got2[0])
-
-    far2, far3 = hop_quarter(after(far1, beside3), 1), hop_quarter(after(far0, beside3), 3)
-    far01 = jnp.stack([far0, far1])
-    far01 = jnp.stack([far01, to_x(after(far01, beside3))], axis=1).reshape(4, 384, 384)
-    out_own = jnp.stack([p[264:] for p in (ring0, beside0, ring1, beside1, ring2, beside2, ring3, beside3)])
-    out_own = jnp.transpose(out_own.reshape(8, 32, 3, 256), (0, 2, 1, 3)).reshape(8, 96, 256)
+    beside3, far1, far3, got1[0], got2[0] = sync(beside3, far1, far3, got1[0], got2[0])
+
+    far2 = hop_quarter(far1, 1)
+    far013 = jnp.stack([far0, far1, far3])
+    far013 = jnp.stack([far013, to_x(far013)], axis=1).reshape(6, 384, 384)
+    got3 = project(ring3, beside3, w_qkv, norm_params)
+    acts, normals, qs, ks, vs, out_own = zip(got0, got1, got2, got3)
+    out_own = jnp.concatenate(out_own)
     out_own = jnp.stack([out_own, to_y(out_own)])
-    got3 = project(ring3, beside3, w_qkv, norm_params)
-    acts, normals, qs, ks, vs = zip(got0, got1, got2, got3)
     mixed, full, q_back = attend(at, qs, ks, vs)
     mixed = list(mixed)
-    *mixed, full, far2, far3, far01, out_own = sync(*mixed, full, far2, far3, far01, out_own)
+    *mixed, full, far2, far013, out_own = sync(*mixed, full, far2, far013, out_own)
 
     mixed = [mixed[0]] + [hop_quarter(mixed[4 - k], k) for k in (3, 2, 1)]
-    far23 = jnp.stack([far2, far3])
-    far23 = jnp.stack([far23, to_x(far23)], axis=1).reshape(4, 384, 384)
+    far2 = jnp.stack([far2, to_x(far2)])
     w_out = place_out(at, out_own, to_core(out_own))
-    *mixed, far23, w_out = sync(*mixed, far23, w_out)
-
-    far01_there, far23_there = to_core(far01), to_core(far23)
+    *mixed, far2, w_out = sync(*mixed, far2, w_out)
+
+    far013_there, far2_there = to_core(far013), to_core(far2)
     two, resid, normal_two, inverse_two, act_three = out_norm(at, patches, mixed, w_out, norm_params)
-    w_mlp = (far01, far23, far01_there, far23_there)
+    w_mlp = (far013, far2, far013_there, far2_there)
     act_three, *w_mlp = sync(act_three, *w_mlp)
 
     act_there = to_y(act_three)
@@ -1073,23 +1111,23 @@
     three_there = to_y(three_send)
     operands = (at, (act_three, act_there), (cotangent, cot_there), (hidden, hidden_there), (wide, wide_there))
     low_keep, low_send = mlp_weights(*operands, (1, 2))
-    low_there = to_core(low_send)
     high_keep, high_send = mlp_weights(*operands, (3, 0))
-    three_there, low_there, high_send = sync(three_there, low_there, high_send)
-
+    three_there, low_send, high_send = sync(three_there, low_send, high_send)
+
+    low_there, high_there = to_core(low_send), to_core(high_send)
+    grad_resid, sums_two, parts, grad_low = norm_out_back(
+        at, three_mine, three_there, cotangent, normal_two, inverse_two, w_out, norm_params
+    )
+    *parts, grad_low = sync(*parts, grad_low)
+
+    grads = [parts[0]] + [hop_quarter(parts[k], k) for k in (1, 2, 3)]
     low_sum = add_low(low_keep, low_there)
+    high_sum = add_low(high_keep, high_there)
     low_x = to_x(low_sum[1])
-    high_there = to_core(high_send)
-    grad_resid, sums_two, parts, w_out_keep, w_out_send = norm_out_back(
-        at, three_mine, three_there, cotangent, normal_two, inverse_two, two, w_out, norm_params
-    )
-    *parts, w_out_send, high_there = sync(*parts, w_out_send, high_there)
-
-    grads = [parts[0]] + [hop_quarter(parts[k], k) for k in (1, 2, 3)]
-    high_sum = add_low(high_keep, high_there)
+    w_out_keep, w_out_send = out_weights(at, grad_low, two)
     out_sum = add_low(w_out_keep, to_core(w_out_send))
     out_sum = add_low(own_y(out_sum), to_y(other_y(out_sum))).reshape(4, 2, HALF, 384)
-    *grads, low_x, high_sum, out_sum = sync(*grads, low_x, high_sum, out_sum)
+    *grads, low_x, high_sum, out_sum, out_send = sync(*grads, low_x, high_sum, out_sum, out_send)
 
     low_half = add_low(low_sum[0], low_x)
     far_got = [hop_quarter(low_half[0], -1), hop_quarter(low_half[1], -2)]
@@ -1098,10 +1136,12 @@
     dqs, dks, dvs = attend_back(at, q_back, ks, vs, full, grads)
     dqs = list(dqs)
     dqs[1], high_half, out_sum = sync(dqs[1], high_half, out_sum)
-
-    last = hop_quarter(jnp.concatenate([high_half[0], out_sum[3]], axis=0), -3)
-    out_got = [hop_quarter(out_sum[1], -1), hop_quarter(out_sum[2], -2), last[384:]]
-    far_got = [*far_got, last[:384]]
+    out_there = to_y(after(out_send, dqs[1]))
+    block_out = (resid + out_mine + out_there.astype(f32)).astype(bf16)
+
+    last = hop_quarter(jnp.concatenate([high_half[0], out_sum[3]], axis=0), 1)
+    far_got.append(last[:384])
+    out_got = [last[384:], hop_quarter(out_sum[1], -1), hop_quarter(out_sum[2], -2)]
     one, sums_one = {}, []
     for ks_here in ((1, 2), (3, 0)):
         keep, send, sums = input_back(*([m[k] for k in ks_here] for m in (normals, dqs, dks, dvs)), w_qkv)
@@ -1111,55 +1151,51 @@
             one[k] = (a, b)
     near_keep, near_send = projections_back(at, acts, dqs, dks, dvs)
     one1 = to_x(one[1][1])
-    one2 = to_x(after(one[2][1], one[0][0]))
-    out_there = to_y(after(out_send, near_keep))
-    block_out = (resid + out_mine + out_there.astype(f32)).astype(bf16)
-    one1, near_send, *far_got = sync(one1, near_send, *far_got)
+    one1, near_send, *far_got, block_out = sync(one1, near_send, *far_got, block_out)
+
+    one_ring = hop_quarter(add_low(one[1][0], one1), 1)
+    one2 = to_x(after(one[2][1], one1))
+    near_sum = add_low(near_keep, to_core(near_send))
+    near_sum = add_low(own_y(near_sum), to_y(other_y(near_sum)))
+    one_ring, one2, near_sum = sync(one_ring, one2, near_sum)
+
+    near_x = to_x(near_sum[3:6])
+    one_ring = hop_quarter(add_low(one_ring, add_low(one[2][0], one2)), 1)
+    one3 = to_x(after(one[3][1], one2))
     far_sum = high_half[1].astype(f32)
     for part in far_got:
         far_sum = far_sum + part.astype(f32)
     out_sum = out_sum[0].astype(f32)
     for part in out_got:
         out_sum = out_sum + part.astype(f32)
-
-    one_ring = hop_quarter(add_low(one[1][0], one1), 1)
-    one_ring = hop_quarter(add_low(one_ring, add_low(one[2][0], one2)), 1)
-    near_sum = add_low(near_keep, to_core(near_send))
-    near_sum = add_low(own_y(near_sum), to_y(other_y(near_sum)))
-    near_x = to_x(near_sum[3:6])
-    one3 = add_low(one[3][0], to_x(after(one[3][1], near_x)))
-    one0 = add_low(one[0][0], to_x(after(one[0][1], near_x)))
-    one_ring = hop_quarter(add_low(one_ring, one3), 1)
-    grad_one = one_ring.astype(f32) + one0.astype(f32)
-    normal_one, inverse_one = layer_stats(patches.astype(f32))
-    patches_grad = grad_resid + layer_back(grad_one, normal_one, inverse_one, norm_params[0])
-    param_grad = jnp.concatenate([sums_one[0][0:2] + sums_one[1][0:2], sums_two[0:2]], axis=0)
-
     near_sum = near_sum[0:3].astype(f32) + near_x.astype(f32)
     near_sum = jnp.concatenate([near_sum.reshape(3 * HALF, 2 * rows), out_sum], axis=0)
     far_own, far_other = by_y(far_sum[:, :rows], far_sum[:, rows:])
     near_own, near_other = by_core(near_sum[:, :rows], near_sum[:, rows:])
     weight_grad = turn(at, far_own, to_y(far_other.astype(bf16)), near_own, to_core(near_other.astype(bf16)))
     squares = jnp.full((4, D), jnp.sum(far_sum * far_sum) + jnp.sum(near_sum * near_sum), f32)
-    sums = jnp.concatenate([param_grad, squares], axis=0)
+    sums = jnp.concatenate([sums_one[0][0:2] + sums_one[1][0:2], sums_two[0:2], squares], axis=0)
     for by in (1, 2):
         sums = sums + hop_quarter(sums, by)
+    sums, one_ring, one3 = sync(sums, one_ring, one3)
+
+    one_ring = hop_quarter(add_low(one_ring, add_low(one[3][0], one3)), 1)
+    one0 = to_x(one[0][1])
     sums = sums + swap(sums, "seq", 1)
-    sums = after(sums, weight_grad)
-    sums = sums + swap(sums, "dp", 2)
+    sums = after(sums + swap(sums, "dp", 2), weight_grad)
     sums = sums + swap(sums, "dp", 1)
-    param_grad = sums[0:4]
-    squares = sums[4, 0] + jnp.sum(param_grad * param_grad)
-    grad_norm = jnp.sqrt(squares)
-    clip = 1.0 / jnp.maximum(grad_norm, 1.0)
-    moments = jnp.transpose(moment_one, (1, 0, 2)), jnp.transpose(moment_two, (1, 0, 2))
-    new_master, *moments = adam_step(master_t, weight_grad * clip, *moments, rate_matrix, weight_decay)
-    new_master, new_copy, new_moment_one, new_moment_two = (
-        jnp.transpose(m, (1, 0, 2)) for m in (new_master, new_master.astype(bf16), *moments)
-    )
-    new_norm_params, new_norm_moment_one, new_norm_moment_two = adam_step(
-        norm_params, param_grad * clip, norm_moment_one, norm_moment_two, rate_vector, 0.0
-    )
+    updated = update(
+        sums,
+        (master_t, weight_grad, jnp.transpose(moment_one, (1, 0, 2)), jnp.transpose(moment_two, (1, 0, 2))),
+        (norm_params, norm_moment_one, norm_moment_two),
+    )
+    new_master, new_copy, new_moment_one, new_moment_two = (jnp.transpose(m, (1, 0, 2)) for m in updated[0:4])
+    new_norm_params, new_norm_moment_one, new_norm_moment_two, grad_norm = updated[4:]
+    grad_norm = grad_norm[0, 0]
+
+    grad_one = one_ring.astype(f32) + one[0][0].astype(f32) + one0.astype(f32)
+    normal_one, inverse_one = layer_stats(patches.astype(f32))
+    patches_grad = grad_resid + layer_back(grad_one, normal_one, inverse_one, norm_params[0])
     return (
         block_out,
         patches_grad,

time: 299 us -> 263 us (0.88)
  Pallas kernels: 108 us -> 76.2 us
  other arithmetic: 30.4 us -> 17.9 us
  local copies, waits for them, and re-layouts: 11.8 us -> 19.7 us
  starting transfers between devices: 68.7 us -> 72.5 us
    pallas_call x18 -> x20, Pallas kernels: 108 us -> 76.2 us  [call(): pl.pallas_call(body, name=name, out_shape=outs, in_specs=ins, out_specs=o...]
    unnamed x118 -> x150, local copies, waits for them, and re-layouts: 6.36 us -> 16.9 us
    reduce_sum x1, other arithmetic: 8.77 us -> 0.24 us  [layer_stats(): spread = jnp.mean(shifted * shifted, axis=-1, keepdims=True)]
    ppermute x22, waiting for transfers between devices: 21 us -> 27.5 us  [hop_quarter(): return lax.ppermute(value, 'seq', pairs)]
    ppermute x38, waiting for transfers between devices: 48.4 us -> 43 us  [swap(): lax.ppermute(value, axis, [(i, i ^ bit) for i in range(lax.axis_size(axis...]
    transpose x1 -> x0, other arithmetic: 4.56 us -> none  [step_small(): jnp.transpose(m, (1, 0, 2))]
    ppermute x22, starting transfers between devices: 36 us -> 39.9 us  [hop_quarter(): return lax.ppermute(value, 'seq', pairs)]
    convert_element_type x12, other arithmetic: 4.82 us -> 8.75 us  [add_low(): return (a.astype(f32) + b.astype(f32)).astype(bf16)]
  transfers between devices with their start and end apart: 60 -> 60, of which waited for: 22 -> 28; matrix products, arithmetic and copies ran while one was open for 11% -> 6% of each run, Pallas kernels for 31% -> 27%
where the time goes in v1:
time: 263 us; the launch traced here: 260 us
  Pallas kernels  76.2 us (29%)
  starting transfers between devices  72.5 us (28%)
  waiting for transfers between devices  70.5 us (27%)
  local copies, waits for them, and re-layouts  19.7 us (7%)
  other arithmetic  17.9 us (7%)
  between operations  3.39 us (1%)
    pallas_call x20, Pallas kernels, call(): pl.pallas_call(body, name=name, out_shape=outs, in_specs=ins, out_specs=o...  76.2 us
    ppermute x38, waiting for transfers between devices, swap(): lax.ppermute(value, axis, [(i, i ^ bit) for i in range(lax.axis_size(axis...  43 us
    ppermute x22, starting transfers between devices, hop_quarter(): return lax.ppermute(value, 'seq', pairs)  39.9 us
    ppermute x38, starting transfers between devices, swap(): lax.ppermute(value, axis, [(i, i ^ bit) for i in range(lax.axis_size(axis...  32.6 us
    ppermute x22, waiting for transfers between devices, hop_quarter(): return lax.ppermute(value, 'seq', pairs)  27.5 us
    unnamed x150, local copies, waits for them, and re-layouts  16.9 us
    convert_element_type x12, other arithmetic, add_low(): return (a.astype(f32) + b.astype(f32)).astype(bf16)  8.75 us
  transfers between devices with their start and end apart: 60, of which 28 were waited for; matrix products, arithmetic and copies ran while one was open for 6% of the time, Pallas kernels for 27%

profile of v1, /device:TPU:0, one launch (start us, length us, event | category | flops | bytes accessed | tf_op | source)
XLA Modules:
  0.0 260.2 jit_solution(8329472455588147901)
XLA Ops:
  3.0 3.1 %collective-permute-start = (bf16[296,768]{1,0:T(8,128)(2,1)S(1)}, bf16[296,768]{1,0:T(8,128)(2,1)S(1)}, u32[]{:S(2)}, u32[]{:S(2)}) collective-permute-start(bf16[296,768]{1,0:T(8,128)(2,1)S(1)} %fusion.16.a_ref), channel_id=1, source_target_pairs={{0,2},{1,3},{2,6},{3,7},{6,4},{7,5},{4,0},{5,1},{8,10},{9,11},{10,... | collective-permute-start | bytes 1363976 | tf_op jit(solution)/shard_map/ppermute | solution.py:44
  10.2 5.0 %collective-permute-done.4 = bf16[384,192]{1,0:T(8,128)(2,1)S(1)} collective-permute-done((bf16[384,192]{1,0:T(8,128)(2,1)S(1)}, bf16[384,192]{1,0:T(8,128)(2,1)S(1)}, u32[]{:S(2)}, u32[]{:S(2)}) %collective-permute-start.4) | collective-permute-done | bytes 147488 | tf_op jit(solution)/shard_map/ppermute | solution.py:54
  15.4 4.9 %collective-permute-done.3 = bf16[144,384]{1,0:T(8,128)(2,1)S(1)} collective-permute-done((bf16[144,384]{1,0:T(8,128)(2,1)S(1)}, bf16[144,384]{1,0:T(8,128)(2,1)S(1)}, u32[]{:S(2)}, u32[]{:S(2)}) %collective-permute-start.3) | collective-permute-done | bytes 110624 | tf_op jit(solution)/shard_map/ppermute | solution.py:54
  22.8 2.6 collective-permute-start.5
  27.4 7.1 %collective-permute-done.5.a_ref = bf16[296,768]{1,0:T(8,128)(2,1)} collective-permute-done((bf16[296,768]{1,0:T(8,128)(2,1)S(1)}, bf16[296,768]{1,0:T(8,128)(2,1)}, u32[]{:S(2)}, u32[]{:S(2)}) %collective-permute-start.5) | collective-permute-done | bytes 454688 | tf_op jit(solution)/shard_map/ppermute | solution.py:44
  56.5 3.4 %norm_project.6 = (bf16[512,768]{1,0:T(8,128)(2,1)S(1)}, bf16[512,768]{1,0:T(8,128)(2,1)S(1)}, bf16[3,256,128]{2,1,0:T(8,128)(2,1)S(1)}, bf16[3,512,128]{2,1,0:T...) custom-call(bf16[296,768]{1,0:T(8,128)(2,1)} %collective-permute-done.5.a_ref, ...), custom_call_target="tpu_custom_call" | custom-call | flops 400000000 | bytes 1440000 | tf_op jit(solution)/shard_map/norm_project/pallas_call | solution.py:362
  62.4 3.0 %norm_project.7 = (bf16[512,768]{1,0:T(8,128)(2,1)S(1)}, bf16[512,768]{1,0:T(8,128)(2,1)S(1)}, bf16[3,256,128]{2,1,0:T(8,128)(2,1)S(1)}, bf16[3,512,128]{2,1,0:T...) custom-call(bf16[296,768]{1,0:T(8,128)(2,1)} %collective-permute-done.9.a_ref, ...), custom_call_target="tpu_custom_call" | custom-call | flops 400000000 | bytes 1440000 | tf_op jit(solution)/shard_map/norm_project/pallas_call | solution.py:362
  67.9 11.9 %collective-permute-start.15 = (bf16[384,384]{1,0:T(8,128)(2,1)S(1)}, bf16[384,384]{1,0:T(8,128)(2,1)S(1)}, u32[]{:S(2)}, u32[]{:S(2)}) collective-permute-start(bf16[384,384]{1,0:T(8,128)(2,1)S(1)} %collective-permute-done.13), channel_id=1, source_target_pairs={{0,2},{1,3},{2,6},{3,7},{6,4},{7,5},{4,0},{5,1},{8,10},{9,11},{10,... | collective-permute-start | bytes 884744 | tf_op jit(solution)/shard_map/ppermute | solution.py:44
  79.9 11.7 %attend.1 = (bf16[256,192]{1,0:T(8,128)(2,1)S(1)}, bf16[256,192]{1,0:T(8,128)(2,1)S(1)}, bf16[256,192]{1,0:T(8,128)(2,1)S(1)}, bf16[256,192]{1,0:T(8,128)(2,1)S(...) custom-call(s32[4]{0:T(128)S(1)} %pad_add_fusion.at_ref, ...), custom_call_target="tpu_custom_call" | custom-call | flops 1200000000 | bytes 4320000 | tf_op jit(solution)/shard_map/attend/pallas_call | solution.py:362
  96.4 2.1 collective-permute-start.19
  98.5 4.3 %collective-permute-done.21 = bf16[384,384]{1,0:T(8,128)(2,1)S(1)} collective-permute-done((bf16[384,384]{1,0:T(8,128)(2,1)S(1)}, bf16[384,384]{1,0:T(8,128)(2,1)S(1)}, u32[]{:S(2)}, u32[]{:S(2)}) %collective-permute-start.21) | collective-permute-done | bytes 294944 | tf_op jit(solution)/shard_map/ppermute | solution.py:54
  103.7 3.0 %place_out.1.w_ref = bf16[4,768,256]{2,1,0:T(8,128)(2,1)S(1)} custom-call(s32[4]{0:T(128)S(1)} %pad_add_fusion.at_ref, bf16[2,8,96,256]{3,2,1,0:T(8,128)(2,1)S(1)} %pad_maximum_fusion.2.own_ref, bf16[2,8,96,256]{3,2,1,0:T(8,128)(2,1)S(1)} %collective-permute-done.22.other_ref), custom_call_target="tpu_custom_call" | custom-call | flops 300000000 | bytes 1080000 | tf_op jit(solution)/shard_map/place_out/pallas_call | solution.py:362
  106.7 2.8 %collective-permute-done.20.m3 = bf16[256,192]{1,0:T(8,128)(2,1)S(1)} collective-permute-done((bf16[256,192]{1,0:T(8,128)(2,1)S(1)}, bf16[256,192]{1,0:T(8,128)(2,1)S(1)}, u32[]{:S(2)}, u32[]{:S(2)}) %collective-permute-start.20) | collective-permute-done | bytes 98336 | tf_op jit(solution)/shard_map/ppermute | solution.py:44
  113.1 5.7 %mlp.2 = (bf16[256,1536]{1,0:T(8,128)(2,1)S(1)}, bf16[256,1536]{1,0:T(8,128)(2,1)S(1)}, f32[256,768]{1,0:T(8,128)S(1)}, f32[256,768]{1,0:T(8,128)S(1)}) custom-call(s32[4]{0:T(128)S(1)} %pad_add_fusion.at_ref, bf16[256,768]{1,0:T(8,128)(2,1)S(1)} %get-tuple-element.237.a_ref.refs_0_, bf16[256,768]{1,0:T(8,128)(2,1)S(1)} %copy-done.1, ...), custom_call_target="tpu_custom_call" | custom-call | flops 800000000 | bytes 2880000 | tf_op jit(solution)/shard_map/mlp/pallas_call | solution.py:362
  119.7 3.0 %collective-permute-done.25.a_ref.refs_1_ = bf16[256,768]{1,0:T(8,128)(2,1)S(1)} collective-permute-done((bf16[256,768]{1,0:T(8,128)(2,1)S(1)}, bf16[256,768]{1,0:T(8,128)(2,1)S(1)}, u32[]{:S(2)}, u32[]{:S(2)}) %collective-permute-start.25) | collective-permute-done | bytes 393248 | tf_op jit(solution)/shard_map/ppermute | solution.py:54
  122.7 5.7 %mlp.3 = (bf16[256,1536]{1,0:T(8,128)(2,1)S(1)}, bf16[256,1536]{1,0:T(8,128)(2,1)S(1)}, bf16[256,768]{1,0:T(8,128)(2,1)S(1)}, bf16[256,768]{1,0:T(8,128)(2,1)S(1)}) custom-call(s32[4]{0:T(128)S(1)} %pad_add_fusion.at_ref, bf16[256,768]{1,0:T(8,128)(2,1)S(1)} %collective-permute-done.25.a_ref.refs_1_, ...), custom_call_target="tpu_custom_call" | custom-call | flops 800000000 | bytes 2880000 | tf_op jit(solution)/shard_map/mlp/pallas_call | solution.py:362
  130.7 3.7 %mlp_weights.2 = (bf16[2,2,384,384]{3,2,1,0:T(8,128)(2,1)S(1)}, bf16[2,2,384,384]{3,2,1,0:T(8,128)(2,1)}) custom-call(s32[4]{0:T(128)S(1)} %pad_add_fusion.at_ref, bf16[256,768]{1,0:T(8,128)(2,1)S(1)} %get-tuple-element.237.a_ref.refs_0_, bf16[256,768]{1,0:T(8,128)(2,1)S(1)} %collective-permute-done.25.a_ref.refs_1_, bf16[256,768]{1,0:T(8,128)(2,1)S(1)} %copy-done.1, ...), custom_call_target="tpu_custom_call" | custom-call | flops 400000000 | bytes 1440000 | tf_op jit(solution)/shard_map/mlp_weights/pallas_call | solution.py:362
  134.4 3.4 %mlp_weights.3 = (bf16[2,2,384,384]{3,2,1,0:T(8,128)(2,1)S(1)}, bf16[2,2,384,384]{3,2,1,0:T(8,128)(2,1)S(1)}) custom-call(s32[4]{0:T(128)S(1)} %pad_add_fusion.at_ref, bf16[256,768]{1,0:T(8,128)(2,1)S(1)} %get-tuple-element.237.a_ref.refs_0_, bf16[256,768]{1,0:T(8,128)(2,1)S(1)} %collective-permute-done.25.a_ref.refs_1_, bf16[256,768]{1,0:T(8,128)(2,1)S(1)} %copy-done.1, ...), custom_call_target="tpu_custom_call" | custom-call | flops 400000000 | bytes 1440000 | tf_op jit(solution)/shard_map/mlp_weights/pallas_call | solution.py:362
  142.1 2.1 out_weights.1
  161.1 6.1 %collective-permute-done.27.refs_10_ = bf16[256,192]{1,0:T(8,128)(2,1)S(1)} collective-permute-done((bf16[256,192]{1,0:T(8,128)(2,1)S(1)}, bf16[256,192]{1,0:T(8,128)(2,1)S(1)}, u32[]{:S(2)}, u32[]{:S(2)}) %collective-permute-start.27) | collective-permute-done | bytes 98336 | tf_op jit(solution)/shard_map/ppermute | solution.py:44
  167.2 2.2 collective-permute-done.31
  173.4 2.3 collective-permute-start.39
  175.8 16.3 %attend_back.1 = (bf16[256,192]{1,0:T(8,128)(2,1)S(1)}, bf16[256,192]{1,0:T(8,128)(2,1)S(1)}, bf16[256,192]{1,0:T(8,128)(2,1)S(1)}, bf16[256,192]{1,0:T(8,128)(2...) custom-call(s32[4]{0:T(128)S(1)} %pad_add_fusion.at_ref, ...), custom_call_target="tpu_custom_call" | custom-call | flops 1600000000 | bytes 5760000 | tf_op jit(solution)/shard_map/attend_back/pallas_call | solution.py:362
  198.6 2.4 projections_back.1
  213.0 3.9 %collective-permute-done.45 = bf16[6,48,384]{2,1,0:T(8,128)(2,1)S(1)} collective-permute-done((bf16[6,48,384]{2,1,0:T(8,128)(2,1)S(1)}, bf16[6,48,384]{2,1,0:T(8,128)(2,1)S(1)}, u32[]{:S(2)}, u32[]{:S(2)}) %collective-permute-start.45) | collective-permute-done | bytes 221216 | tf_op jit(solution)/shard_map/ppermute | solution.py:54
  217.0 2.2 collective-permute-done.42
  219.2 2.8 %collective-permute-done.43 = bf16[256,768]{1,0:T(8,128)(2,1)S(1)} collective-permute-done((bf16[256,768]{1,0:T(8,128)(2,1)S(1)}, bf16[256,768]{1,0:T(8,128)(2,1)S(1)}, u32[]{:S(2)}, u32[]{:S(2)}) %collective-permute-start.43) | collective-permute-done | bytes 393248 | tf_op jit(solution)/shard_map/ppermute | solution.py:54
  223.2 3.6 %collective-permute-done.46 = bf16[3,48,384]{2,1,0:T(8,128)(2,1)S(1)} collective-permute-done((bf16[3,48,384]{2,1,0:T(8,128)(2,1)S(1)}, bf16[3,48,384]{2,1,0:T(8,128)(2,1)S(1)}, u32[]{:S(2)}, u32[]{:S(2)}) %collective-permute-start.46) | collective-permute-done | bytes 110624 | tf_op jit(solution)/shard_map/ppermute | solution.py:54
  238.1 3.3 %collective-permute-done.50 = f32[8,768]{1,0:T(8,128)S(1)} collective-permute-done((f32[8,768]{1,0:T(8,128)S(1)}, f32[8,768]{1,0:T(8,128)S(1)}, u32[]{:S(2)}, u32[]{:S(2)}) %collective-permute-start.50) | collective-permute-done | bytes 24608 | tf_op jit(solution)/shard_map/ppermute | solution.py:44
  244.4 2.7 %collective-permute-done.55 = f32[8,768]{1,0:T(8,128)S(1)} collective-permute-done((f32[8,768]{1,0:T(8,128)S(1)}, f32[8,768]{1,0:T(8,128)S(1)}, u32[]{:S(2)}, u32[]{:S(2)}) %collective-permute-start.55) | collective-permute-done | bytes 24608 | tf_op jit(solution)/shard_map/ppermute | solution.py:54
  252.2 3.6 %update.1 = (f32[12,192,96]{2,1,0:T(8,128)}, bf16[12,192,96]{2,1,0:T(8,128)(2,1)}, f32[12,192,96]{2,1,0:T(8,128)}, f32[12,192,96]{2,1,0:T(8,128)}, f32[4,768]{1,...) custom-call(f32[8,768]{1,0:T(8,128)S(1)} %add.169.sums_ref, f32[12,192,96]{2,1,0:T(8,128)S(1)} %bitcast.89, ...), custom_call_target="tpu_custom_call" | custom-call | flops 400000000 | bytes 1440000 | tf_op jit(solution)/shard_map/update/pallas_call | solution.py:362
  257.8 2.3 fusion.11
  (333 shorter events, 114.7 us)
Async XLA Ops:
  3.0 17.4 %collective-permute-start = (bf16[296,768]{1,0:T(8,128)(2,1)S(1)}, bf16[296,768]{1,0:T(8,128)(2,1)S(1)}, u32[]{:S(2)}, u32[]{:S(2)}) collective-permute-start(bf16[296,768]{1,0:T(8,128)(2,1)S(1)} %fusion.16.a_ref), channel_id=1, source_target_pairs={{0,2},{1,3},{2,6},{3,7},{6,4},{7,5},{4,0},{5,1},{8,10},{9,11},{10,... | collective-permute-start | bytes 1363976 | tf_op jit(solution)/shard_map/ppermute | solution.py:44
  6.1 14.3 %collective-permute-start.1 = (bf16[296,768]{1,0:T(8,128)(2,1)S(1)}, bf16[296,768]{1,0:T(8,128)(2,1)S(1)}, u32[]{:S(2)}, u32[]{:S(2)}) collective-permute-start(bf16[296,768]{1,0:T(8,128)(2,1)S(1)} %fusion.16.a_ref), channel_id=1, source_target_pairs={{0,1},{1,0},{2,3},{3,2},{4,5},{5,4},{6,7},{7,6},{8,9},{9,8},{10,11... | collective-permute-start | bytes 1363976 | tf_op jit(solution)/shard_map/ppermute | solution.py:54
  9.5 10.8 %collective-permute-start.3 = (bf16[144,384]{1,0:T(8,128)(2,1)S(1)}, bf16[144,384]{1,0:T(8,128)(2,1)S(1)}, u32[]{:S(2)}, u32[]{:S(2)}) collective-permute-start(bf16[144,384]{1,0:T(8,128)(2,1)S(1)} %pad_maximum_fusion.11), channel_id=1, source_target_pairs={{0,1},{1,0},{2,3},{3,2},{4,5},{5,4},{6,7},{7,6},{8,9},{9,8},{10,11... | collective-permute-start | bytes 331784 | tf_op jit(solution)/shard_map/ppermute | solution.py:54
  22.8 11.7 %collective-permute-start.5 = (bf16[296,768]{1,0:T(8,128)(2,1)S(1)}, bf16[296,768]{1,0:T(8,128)(2,1)}, u32[]{:S(2)}, u32[]{:S(2)}) collective-permute-start(bf16[296,768]{1,0:T(8,128)(2,1)S(1)} %collective-permute-done.a_ref), channel_id=1, source_target_pairs={{0,2},{1,3},{2,6},{3,7},{6,4},{7,5},{4,0},{5,1},{8,10},{9,11},{10,... | collective-permute-start | bytes 1363976 | tf_op jit(solution)/shard_map/ppermute | solution.py:44
  25.4 10.4 %collective-permute-start.6 = (bf16[296,768]{1,0:T(8,128)(2,1)S(1)}, bf16[296,768]{1,0:T(8,128)(2,1)S(1)}, u32[]{:S(2)}, u32[]{:S(2)}) collective-permute-start(bf16[296,768]{1,0:T(8,128)(2,1)S(1)} %collective-permute-done.a_ref), channel_id=1, source_target_pairs={{0,1},{1,0},{2,3},{3,2},{4,5},{5,4},{6,7},{7,6},{8,9},{9,8},{10,11... | collective-permute-start | bytes 1363976 | tf_op jit(solution)/shard_map/ppermute | solution.py:54
  37.3 10.8 %collective-permute-start.9 = (bf16[296,768]{1,0:T(8,128)(2,1)}, bf16[296,768]{1,0:T(8,128)(2,1)}, u32[]{:S(2)}, u32[]{:S(2)}) collective-permute-start(bf16[296,768]{1,0:T(8,128)(2,1)} %collective-permute-done.5.a_ref), channel_id=1, source_target_pairs={{0,2},{1,3},{2,6},{3,7},{6,4},{7,5},{4,0},{5,1},{8,10},{9,11},{10,... | collective-permute-start | bytes 1363976 | tf_op jit(solution)/shard_map/ppermute | solution.py:44
  37.8 10.4 %collective-permute-start.10 = (bf16[296,768]{1,0:T(8,128)(2,1)}, bf16[296,768]{1,0:T(8,128)(2,1)}, u32[]{:S(2)}, u32[]{:S(2)}) collective-permute-start(bf16[296,768]{1,0:T(8,128)(2,1)} %collective-permute-done.5.a_ref), channel_id=1, source_target_pairs={{0,1},{1,0},{2,3},{3,2},{4,5},{5,4},{6,7},{7,6},{8,9},{9,8},{10,11... | collective-permute-start | bytes 1363976 | tf_op jit(solution)/shard_map/ppermute | solution.py:54
  48.1 13.1 %collective-permute-start.12 = (bf16[296,768]{1,0:T(8,128)(2,1)}, bf16[296,768]{1,0:T(8,128)(2,1)S(1)}, u32[]{:S(2)}, u32[]{:S(2)}) collective-permute-start(bf16[296,768]{1,0:T(8,128)(2,1)} %collective-permute-done.9.a_ref), channel_id=1, source_target_pairs={{0,1},{1,0},{2,3},{3,2},{4,5},{5,4},{6,7},{7,6},{8,9},{9,8},{10,11... | collective-permute-start | bytes 1363976 | tf_op jit(solution)/shard_map/ppermute | solution.py:54
  61.5 30.3 %collective-permute-start.16 = (bf16[3,384,384]{2,1,0:T(8,128)(2,1)S(1)}, bf16[3,384,384]{2,1,0:T(8,128)(2,1)S(1)}, u32[]{:S(2)}, u32[]{:S(2)}) collective-permute-start(bf16[3,384,384]{2,1,0:T(8,128)(2,1)S(1)} %get-tuple-element.353), channel_id=1, source_target_pairs={{0,1},{1,0},{2,3},{3,2},{4,5},{5,4},{6,7},{7,6},{8,9},{9,8},{10,11... | collective-permute-start | bytes 2654216 | tf_op jit(solution)/shard_map/ppermute | solution.py:54
  67.2 24.5 %collective-permute-start.17 = (bf16[8,96,256]{2,1,0:T(8,128)(2,1)S(1)}, bf16[8,96,256]{2,1,0:T(8,128)(2,1)S(1)}, u32[]{:S(2)}, u32[]{:S(2)}) collective-permute-start(bf16[8,96,256]{2,1,0:T(8,128)(2,1)S(1)} %constant_dynamic-update-slice_fusion), channel_id=1, source_target_pairs={{0,16},{8,24},{16,0},{24,8},{1,17},{9,25},{17,1},{25,9},{2,18},{10... | collective-permute-start | bytes 1179656 | tf_op jit(solution)/shard_map/ppermute | solution.py:54
  67.9 25.3 %collective-permute-start.15 = (bf16[384,384]{1,0:T(8,128)(2,1)S(1)}, bf16[384,384]{1,0:T(8,128)(2,1)S(1)}, u32[]{:S(2)}, u32[]{:S(2)}) collective-permute-start(bf16[384,384]{1,0:T(8,128)(2,1)S(1)} %collective-permute-done.13), channel_id=1, source_target_pairs={{0,2},{1,3},{2,6},{3,7},{6,4},{7,5},{4,0},{5,1},{8,10},{9,11},{10,... | collective-permute-start | bytes 884744 | tf_op jit(solution)/shard_map/ppermute | solution.py:44
  93.3 18.3 %collective-permute-start.23 = (bf16[6,384,384]{2,1,0:T(8,128)(2,1)S(1)}, bf16[6,384,384]{2,1,0:T(8,128)(2,1)S(1)}, u32[]{:S(2)}, u32[]{:S(2)}) collective-permute-start(bf16[6,384,384]{2,1,0:T(8,128)(2,1)S(1)} %bitcast.86), channel_id=1, source_target_pairs={{0,8},{8,0},{16,24},{24,16},{1,9},{9,1},{17,25},{25,17},{2,10},{10... | collective-permute-start | bytes 5308424 | tf_op jit(solution)/shard_map/ppermute | solution.py:54
  93.3 10.4 %collective-permute-start.22 = (bf16[2,8,96,256]{3,2,1,0:T(8,128)(2,1)S(1)}, bf16[2,8,96,256]{3,2,1,0:T(8,128)(2,1)S(1)}, u32[]{:S(2)}, u32[]{:S(2)}) collective-permute-start(bf16[2,8,96,256]{3,2,1,0:T(8,128)(2,1)S(1)} %pad_maximum_fusion.2.own_ref), channel_id=1, source_target_pairs={{0,8},{8,0},{16,24},{24,16},{1,9},{9,1},{17,25},{25,17},{2,10},{10... | collective-permute-start | bytes 2359304 | tf_op jit(solution)/shard_map/ppermute | solution.py:54
  94.7 12.0 %collective-permute-start.18 = (bf16[256,192]{1,0:T(8,128)(2,1)S(1)}, bf16[256,192]{1,0:T(8,128)(2,1)S(1)}, u32[]{:S(2)}, u32[]{:S(2)}) collective-permute-start(bf16[256,192]{1,0:T(8,128)(2,1)S(1)} %get-tuple-element.224), channel_id=1, source_target_pairs={{0,4},{1,5},{2,0},{3,1},{6,2},{7,3},{4,6},{5,7},{8,12},{9,13},{10,... | collective-permute-start | bytes 294920 | tf_op jit(solution)/shard_map/ppermute | solution.py:44
  111.5 11.2 %collective-permute-start.25 = (bf16[256,768]{1,0:T(8,128)(2,1)S(1)}, bf16[256,768]{1,0:T(8,128)(2,1)S(1)}, u32[]{:S(2)}, u32[]{:S(2)}) collective-permute-start(bf16[256,768]{1,0:T(8,128)(2,1)S(1)} %get-tuple-element.237.a_ref.refs_0_), channel_id=1, source_target_pairs={{0,16},{8,24},{16,0},{24,8},{1,17},{9,25},{17,1},{25,9},{2,18},{10... | collective-permute-start | bytes 1179656 | tf_op jit(solution)/shard_map/ppermute | solution.py:54
  129.2 10.3 %collective-permute-start.26 = (bf16[256,768]{1,0:T(8,128)(2,1)S(1)}, bf16[256,768]{1,0:T(8,128)(2,1)S(1)}, u32[]{:S(2)}, u32[]{:S(2)}) collective-permute-start(bf16[256,768]{1,0:T(8,128)(2,1)S(1)} %get-tuple-element.248), channel_id=1, source_target_pairs={{0,16},{8,24},{16,0},{24,8},{1,17},{9,25},{17,1},{25,9},{2,18},{10... | collective-permute-start | bytes 1179656 | tf_op jit(solution)/shard_map/ppermute | solution.py:54
  139.5 10.8 %collective-permute-start.30 = (bf16[2,2,384,384]{3,2,1,0:T(8,128)(2,1)}, bf16[2,2,384,384]{3,2,1,0:T(8,128)(2,1)}, u32[]{:S(2)}, u32[]{:S(2)}) collective-permute-start(bf16[2,2,384,384]{3,2,1,0:T(8,128)(2,1)} %get-tuple-element.268), channel_id=1, source_target_pairs={{0,8},{8,0},{16,24},{24,16},{1,9},{9,1},{17,25},{25,17},{2,10},{10... | collective-permute-start | bytes 3538952 | tf_op jit(solution)/shard_map/ppermute | solution.py:54
  145.0 14.3 %collective-permute-start.32 = (bf16[2,2,384,384]{3,2,1,0:T(8,128)(2,1)}, bf16[2,2,384,384]{3,2,1,0:T(8,128)(2,1)}, u32[]{:S(2)}, u32[]{:S(2)}) collective-permute-start(bf16[2,2,384,384]{3,2,1,0:T(8,128)(2,1)} %copy-done.60), channel_id=1, source_target_pairs={{0,8},{8,0},{16,24},{24,16},{1,9},{9,1},{17,25},{25,17},{2,10},{10... | collective-permute-start | bytes 3538952 | tf_op jit(solution)/shard_map/ppermute | solution.py:54
  153.8 15.6 %collective-permute-start.31 = (bf16[2,384,384]{2,1,0:T(8,128)(2,1)}, bf16[2,384,384]{2,1,0:T(8,128)(2,1)}, u32[]{:S(2)}, u32[]{:S(2)}) collective-permute-start(bf16[2,384,384]{2,1,0:T(8,128)(2,1)} %slice_bitcast_fusion.1), channel_id=1, source_target_pairs={{0,1},{1,0},{2,3},{3,2},{4,5},{5,4},{6,7},{7,6},{8,9},{9,8},{10,11... | collective-permute-start | bytes 1769480 | tf_op jit(solution)/shard_map/ppermute | solution.py:54
  154.3 12.9 %collective-permute-start.27 = (bf16[256,192]{1,0:T(8,128)(2,1)S(1)}, bf16[256,192]{1,0:T(8,128)(2,1)S(1)}, u32[]{:S(2)}, u32[]{:S(2)}) collective-permute-start(bf16[256,192]{1,0:T(8,128)(2,1)S(1)} %copy-done.66), channel_id=1, source_target_pairs={{0,2},{1,3},{2,6},{3,7},{6,4},{7,5},{4,0},{5,1},{8,10},{9,11},{10,... | collective-permute-start | bytes 294920 | tf_op jit(solution)/shard_map/ppermute | solution.py:44
  154.4 12.8 %collective-permute-start.28 = (bf16[256,192]{1,0:T(8,128)(2,1)S(1)}, bf16[256,192]{1,0:T(8,128)(2,1)S(1)}, u32[]{:S(2)}, u32[]{:S(2)}) collective-permute-start(bf16[256,192]{1,0:T(8,128)(2,1)S(1)} %get-tuple-element.265), channel_id=1, source_target_pairs={{0,6},{1,7},{2,4},{3,5},{6,0},{7,1},{4,2},{5,3},{8,14},{9,15},{10,... | collective-permute-start | bytes 294920 | tf_op jit(solution)/shard_map/ppermute | solution.py:44
  169.5 22.7 %collective-permute-start.35 = (bf16[2,384,384]{2,1,0:T(8,128)(2,1)S(1)}, bf16[2,384,384]{2,1,0:T(8,128)(2,1)S(1)}, u32[]{:S(2)}, u32[]{:S(2)}) collective-permute-start(bf16[2,384,384]{2,1,0:T(8,128)(2,1)S(1)} %slice_bitcast_fusion.2), channel_id=1, source_target_pairs={{0,1},{1,0},{2,3},{3,2},{4,5},{5,4},{6,7},{7,6},{8,9},{9,8},{10,11... | collective-permute-start | bytes 1769480 | tf_op jit(solution)/shard_map/ppermute | solution.py:54
  170.1 22.0 %collective-permute-start.36 = (bf16[4,48,384]{2,1,0:T(8,128)(2,1)S(1)}, bf16[4,48,384]{2,1,0:T(8,128)(2,1)S(1)}, u32[]{:S(2)}, u32[]{:S(2)}) collective-permute-start(bf16[4,48,384]{2,1,0:T(8,128)(2,1)S(1)} %slice_bitcast_fusion.6), channel_id=1, source_target_pairs={{0,1},{1,0},{2,3},{3,2},{4,5},{5,4},{6,7},{7,6},{8,9},{9,8},{10,11... | collective-permute-start | bytes 442376 | tf_op jit(solution)/shard_map/ppermute | solution.py:54
  173.0 32.6 %collective-permute-start.38 = (bf16[384,384]{1,0:T(8,128)(2,1)S(1)}, bf16[384,384]{1,0:T(8,128)(2,1)S(1)}, u32[]{:S(2)}, u32[]{:S(2)}) collective-permute-start(bf16[384,384]{1,0:T(8,128)(2,1)S(1)} %get-tuple-element.355), channel_id=1, source_target_pairs={{0,4},{1,5},{2,0},{3,1},{6,2},{7,3},{4,6},{5,7},{8,12},{9,13},{10,... | collective-permute-start | bytes 884744 | tf_op jit(solution)/shard_map/ppermute | solution.py:44
  173.4 33.1 %collective-permute-start.39 = (bf16[384,384]{1,0:T(8,128)(2,1)S(1)}, bf16[384,384]{1,0:T(8,128)(2,1)S(1)}, u32[]{:S(2)}, u32[]{:S(2)}) collective-permute-start(bf16[384,384]{1,0:T(8,128)(2,1)S(1)} %get-tuple-element.354), channel_id=1, source_target_pairs={{0,6},{1,7},{2,4},{3,5},{6,0},{7,1},{4,2},{5,3},{8,14},{9,15},{10,... | collective-permute-start | bytes 884744 | tf_op jit(solution)/shard_map/ppermute | solution.py:44
  193.1 10.9 %collective-permute-start.41 = (bf16[256,768]{1,0:T(8,128)(2,1)S(1)}, bf16[256,768]{1,0:T(8,128)(2,1)S(1)}, u32[]{:S(2)}, u32[]{:S(2)}) collective-permute-start(bf16[256,768]{1,0:T(8,128)(2,1)S(1)} %copy-done.62), channel_id=1, source_target_pairs={{0,16},{8,24},{16,0},{24,8},{1,17},{9,25},{17,1},{25,9},{2,18},{10... | collective-permute-start | bytes 1179656 | tf_op jit(solution)/shard_map/ppermute | solution.py:54
  195.5 11.0 %collective-permute-start.37 = (bf16[256,768]{1,0:T(8,128)(2,1)S(1)}, bf16[256,768]{1,0:T(8,128)(2,1)S(1)}, u32[]{:S(2)}, u32[]{:S(2)}) collective-permute-start(bf16[256,768]{1,0:T(8,128)(2,1)S(1)} %get-tuple-element.289), channel_id=1, source_target_pairs={{0,1},{1,0},{2,3},{3,2},{4,5},{5,4},{6,7},{7,6},{8,9},{9,8},{10,11... | collective-permute-start | bytes 1179656 | tf_op jit(solution)/shard_map/ppermute | solution.py:54
  205.5 50.8 %collective-permute-start.54 = (bf16[256,768]{1,0:T(8,128)(2,1)}, bf16[256,768]{1,0:T(8,128)(2,1)}, u32[]{:S(2)}, u32[]{:S(2)}) collective-permute-start(bf16[256,768]{1,0:T(8,128)(2,1)} %get-tuple-element.337), channel_id=1, source_target_pairs={{0,1},{1,0},{2,3},{3,2},{4,5},{5,4},{6,7},{7,6},{8,9},{9,8},{10,11... | collective-permute-start | bytes 1179656 | tf_op jit(solution)/shard_map/ppermute | solution.py:54
  208.6 10.6 %collective-permute-start.42 = (bf16[256,768]{1,0:T(8,128)(2,1)S(1)}, bf16[256,768]{1,0:T(8,128)(2,1)S(1)}, u32[]{:S(2)}, u32[]{:S(2)}) collective-permute-start(bf16[256,768]{1,0:T(8,128)(2,1)S(1)} %add_convert_fusion.8), channel_id=1, source_target_pairs={{0,2},{1,3},{2,6},{3,7},{6,4},{7,5},{4,0},{5,1},{8,10},{9,11},{10,... | collective-permute-start | bytes 1179656 | tf_op jit(solution)/shard_map/ppermute | solution.py:44
  209.7 12.3 %collective-permute-start.43 = (bf16[256,768]{1,0:T(8,128)(2,1)S(1)}, bf16[256,768]{1,0:T(8,128)(2,1)S(1)}, u32[]{:S(2)}, u32[]{:S(2)}) collective-permute-start(bf16[256,768]{1,0:T(8,128)(2,1)S(1)} %get-tuple-element.325), channel_id=1, source_target_pairs={{0,1},{1,0},{2,3},{3,2},{4,5},{5,4},{6,7},{7,6},{8,9},{9,8},{10,11... | collective-permute-start | bytes 1179656 | tf_op jit(solution)/shard_map/ppermute | solution.py:54
  236.6 11.9 %collective-permute-start.57 = (bf16[384,192]{1,0:T(8,128)(2,1)S(1)}, bf16[384,192]{1,0:T(8,128)(2,1)S(1)}, u32[]{:S(2)}, u32[]{:S(2)}) collective-permute-start(bf16[384,192]{1,0:T(8,128)(2,1)S(1)} %select_convert_fusion), channel_id=1, source_target_pairs={{0,16},{8,24},{16,0},{24,8},{1,17},{9,25},{17,1},{25,9},{2,18},{10... | collective-permute-start | bytes 442376 | tf_op jit(solution)/shard_map/ppermute | solution.py:54
  241.8 14.5 %collective-permute-start.53 = (bf16[256,768]{1,0:T(8,128)(2,1)S(1)}, bf16[256,768]{1,0:T(8,128)(2,1)S(1)}, u32[]{:S(2)}, u32[]{:S(2)}) collective-permute-start(bf16[256,768]{1,0:T(8,128)(2,1)S(1)} %add_convert_fusion.4), channel_id=1, source_target_pairs={{0,2},{1,3},{2,6},{3,7},{6,4},{7,5},{4,0},{5,1},{8,10},{9,11},{10,... | collective-permute-start | bytes 1179656 | tf_op jit(solution)/shard_map/ppermute | solution.py:44
  (102 other events, 718.2 us)
